TPU v7x, 512 devices: a whole 4x8x8 slice. The times are simulated.
512 devices in a mesh: req: 128 (over z, y, core), tp: 4 (over x).
Axes of the slice: x: 4, y: 8, z: 8, core: 2. Of those that a mesh axis runs over, the one named last changes fastest.
Arguments:
- prompt_query: bfloat16 [32768, 2048], P('req', 'tp')
- prompt_key_value: bfloat16 [32768, 4, 256], P('req', 'tp')
- prompt_segment_index: int32 [128, 256], P('req'), may hold values from 0 to 3, never falling along the last dimension, each value on 1 to 128 neighbouring positions
- decoder_query: bfloat16 [256, 2048], P('req', 'tp')
- decoder_key_value: bfloat16 [256, 4, 256], P('req', 'tp')
- key_value_cache: bfloat16 [256, 512, 4, 256], P('req', None, 'tp')
- live_cache_length: int32 [256], P('req'), may hold values from 128 to 512, as said below
- rebuild_hidden_state: bfloat16 [16384, 2048], P('req'), may hold values from -6 to 6
- owner_dest: int32 [128, 128], P('req'), may hold values from -1 to 127, as said below
- miss_pos: int32 [128, 128], P('req'), may hold values from -1 to 1023, as said below
- key_value_weight: bfloat16 [2048, 4, 256], P(None, 'tp'), may hold values from -0.125 to 0.125
- out_weight: bfloat16 [2048, 2048], P('tp'), may hold values from -0.125 to 0.125
Outputs:
- prompt_out: bfloat16 [32768, 2048], P('req', 'tp')
- dec_out: bfloat16 [256, 2048], P('req', 'tp')
Inputs may be any that keep to these rules, and one draw needn't show every extreme that they name: `prompt_segment_index`: each device's numbers never fall along the row; each prompt has 1 to 128 tokens and one has exactly that many. Positions 0 to live_cache_length - 1 of a decoder are live; some decoder has exactly 512. Row r of device o's list goes to device owner_dest[o, r], or nowhere if -1. The rows of one device going to one device are exactly rows g * 2 to g * 2 + 1 of one block g, all sent or all -1; some device receives 2 rows from each of 64 devices. A row r that device o sends to device e fills cache slot miss_pos[e, r] = decoder * 512 + position of device e; miss_pos[e, r] is -1 exactly where no device sends row r to e. The live slots of one device are distinct and below that decoder's live_cache_length.
All inputs are finite; a program needn't handle non-finite values.
Results may differ from a plain program's by a relative error of at most 0.019.
Values may be sent and summed in bfloat16 or wider, within the bound.
No kernel may reach another device: no remote copies, remote signals or barrier semaphores. Data moves between devices by JAX's collectives and lax.ppermute only.
A program may use at most 64 MiB of HBM per device.

v0:
```python
import jax
import jax.numpy as jnp
from jax import lax
from jax.sharding import PartitionSpec as P

CAP = 2


ROPE_BASE = 600000.0


def rotate(key_rows, position):
    half_width = key_rows.shape[-1] // 2
    frequency = ROPE_BASE ** (-2.0 * jnp.arange(half_width, dtype=jnp.float32) / key_rows.shape[-1])
    angles = position.astype(jnp.float32)[:, None, None] * frequency[None, None, :]
    front_half = key_rows[..., :half_width]
    back_half = key_rows[..., half_width:]
    cosine = jnp.cos(angles)
    sine_part = jnp.sin(angles)
    return jnp.concatenate(
        [front_half * cosine - back_half * sine_part, back_half * cosine + front_half * sine_part],
        axis=-1,
    )


def normalize(score_parts, self_score):
    row_peak = self_score
    for scores in score_parts:
        row_peak = jnp.maximum(row_peak, jnp.max(scores, axis=-1))
    own_exp = jnp.exp(self_score - row_peak)
    row_total = own_exp
    exponents = []
    for scores in score_parts:
        exponent = jnp.exp(scores - row_peak[..., None])
        exponents.append(exponent)
        row_total = row_total + jnp.sum(exponent, axis=-1)
    return (
        (own_exp / row_total).astype(jnp.bfloat16),
        [(exponent / row_total[..., None]).astype(jnp.bfloat16) for exponent in exponents],
    )


def shards(
    prompt_query,
    prompt_key_value,
    prompt_segment_index,
    decoder_query,
    decoder_key_value,
    key_value_cache,
    live_cache_length,
    rebuild_hidden_state,
    owner_dest,
    miss_pos,
    key_value_weight,
    out_weight,
):
    head_width = prompt_key_value.shape[-1] // 2
    local_heads = prompt_key_value.shape[1]
    queries_per_group = prompt_query.shape[1] // (local_heads * head_width)
    peer_count = lax.axis_size("req")
    decoders, cache_len = (key_value_cache.shape[0], key_value_cache.shape[1])
    prompt_rows = prompt_query.shape[0]
    logit_scale = head_width ** (-0.5)
    rebuilt_rows = jnp.dot(
        rebuild_hidden_state,
        key_value_weight.reshape(key_value_weight.shape[0], -1),
        preferred_element_type=jnp.float32,
    ).astype(jnp.bfloat16)
    row_order = jnp.arange(rebuilt_rows.shape[0], dtype=jnp.int32)
    target_position = owner_dest[0]
    where_to = jnp.where(target_position >= 0, target_position, peer_count)
    slot_lane = row_order % CAP
    send_rows = (
        jnp.zeros((peer_count, CAP, rebuilt_rows.shape[1]), jnp.bfloat16)
        .at[where_to, slot_lane]
        .set(rebuilt_rows, mode="drop")
    )
    send_index = (
        jnp.full((peer_count, CAP), -1, jnp.int32)
        .at[where_to, slot_lane]
        .set(row_order, mode="drop")
    )
    got_rows, got_index = (
        lax.all_to_all(send_rows, "req", split_axis=0, concat_axis=0, tiled=True),
        lax.all_to_all(send_index, "req", split_axis=0, concat_axis=0, tiled=True),
    )
    got_rows = got_rows.reshape(-1, local_heads, 2 * head_width)
    got_index = got_index.reshape(-1)
    cache_slot = jnp.where(got_index >= 0, miss_pos[0][jnp.maximum(got_index, 0)], -1)
    rotated = rotate(
        got_rows[..., :head_width].astype(jnp.float32), jnp.maximum(cache_slot, 0) % cache_len
    ).astype(jnp.bfloat16)
    got_rows = jnp.concatenate([rotated, got_rows[..., head_width:]], axis=-1)
    query_rows = decoder_query.reshape(decoders, local_heads, queries_per_group, head_width)
    self_score = (
        jnp.einsum(
            "siwr,sir->siw",
            query_rows,
            decoder_key_value[..., :head_width],
            preferred_element_type=jnp.float32,
        )
        * logit_scale
    )
    alive_mask = jnp.arange(cache_len)[None, :] < live_cache_length[:, None]
    total_slots = decoders * cache_len
    target_slot = jnp.where(cache_slot >= 0, cache_slot, total_slots)
    updated_cache = (
        key_value_cache.reshape(total_slots, local_heads, 2 * head_width)
        .at[target_slot]
        .set(got_rows, mode="drop")
        .reshape(key_value_cache.shape)
    )
    cache_score = (
        jnp.einsum(
            "bkgd,bckd->bkgc",
            query_rows,
            updated_cache[..., :head_width],
            preferred_element_type=jnp.float32,
        )
        * logit_scale
    )
    cache_score = jnp.where(alive_mask[:, None, None, :], cache_score, -jnp.inf)
    own_weight, weight_list = normalize([cache_score], self_score)
    mixture = jnp.einsum(
        "bkgc,bckd->bkgd",
        weight_list[0],
        updated_cache[..., head_width:],
        preferred_element_type=jnp.float32,
    )
    mixture = mixture + own_weight.astype(jnp.float32)[..., None] * decoder_key_value[
        :, :, None, head_width:
    ].astype(jnp.float32)
    decoder_attention = mixture.astype(jnp.bfloat16).reshape(decoders, -1)
    prompt_queries = prompt_query.reshape(prompt_rows, local_heads, queries_per_group, head_width)
    scores = (
        jnp.einsum(
            "ikgd,jkd->kgij",
            prompt_queries,
            prompt_key_value[..., :head_width],
            preferred_element_type=jnp.float32,
        )
        * logit_scale
    )
    segment = prompt_segment_index[0]
    positions = jnp.arange(prompt_rows)
    allowed = (segment[:, None] == segment[None, :]) & (positions[None, :] <= positions[:, None])
    scores = jnp.where(allowed, scores, -jnp.inf)
    row_peak = jnp.max(scores, axis=-1, keepdims=True)
    exponent = jnp.exp(scores - row_peak)
    weight = (exponent / jnp.sum(exponent, axis=-1, keepdims=True)).astype(jnp.bfloat16)
    prompt_attention = jnp.einsum(
        "kgij,jkd->ikgd",
        weight,
        prompt_key_value[..., head_width:],
        preferred_element_type=jnp.float32,
    )
    prompt_attention = prompt_attention.astype(jnp.bfloat16).reshape(prompt_rows, -1)
    combined = jnp.concatenate([prompt_attention, decoder_attention], axis=0)
    partial_sums = jnp.dot(combined, out_weight, preferred_element_type=jnp.float32)
    summed = lax.psum_scatter(
        partial_sums.astype(jnp.bfloat16), "tp", scatter_dimension=1, tiled=True
    )
    return (summed[:prompt_rows], summed[prompt_rows:])


def solution(mesh):
    in_specs = (
        P("req", "tp"),
        P("req", "tp", None),
        P("req", None),
        P("req", "tp"),
        P("req", "tp", None),
        P("req", None, "tp", None),
        P("req"),
        P("req", None),
        P("req", None),
        P("req", None),
        P(None, "tp", None),
        P("tp", None),
    )
    out_specs = (P("req", "tp"), P("req", "tp"))
    return jax.shard_map(shards, mesh=mesh, in_specs=in_specs, out_specs=out_specs, check_vma=False)
```

profile of v0, /device:TPU:8, one launch (start us, length us, event | category | flops | bytes accessed | tf_op | source)
XLA Modules:
  0.0 113.5 jit_solution(9934487164400505404)
XLA Ops:
  7.2 0.0 copy-start
  7.2 0.0 copy-start.5
  7.2 0.0 copy-start.6
  7.2 0.0 copy-start.7
  7.2 0.0 copy-start.8
  7.2 0.0 copy-start.9
  7.2 0.0 copy-start.10
  7.2 0.8 fusion.38
  8.1 6.4 %scatter_fusion = s32[128,2]{0,1:T(2,128)S(1)} fusion(s32[128,2]{0,1:T(2,128)S(1)} %broadcast_in_dim.61, s32[128]{0:T(128)S(1)} %fusion.38, s32[128]{0:T(128)S(1)} %iota.26), kind=kCustom, calls=%fused_computation.1 | custom fusion | bytes 2560 | tf_op jit(solution)/shard_map/scatter | solution.py:81
  14.4 0.7 copy.38
  15.2 17.4 %all-to-all-start = ((s32[128,1,2]{2,1,0:T(1,128)}), s32[128,1,2]{2,1,0:T(1,128)S(1)}, u32[]{:S(2)}, u32[]{:S(2)}) async-start(s32[128,1,2]{2,1,0:T(1,128)} %copy.38), calls=%async_computation | async-start | bytes 131072 | tf_op jit(solution)/shard_map/all_to_all | solution.py:85
  32.5 0.0 copy-done.9
  32.6 0.0 copy-done.8
  32.6 0.0 copy-done.10
  32.6 0.1 iota_compare_fusion.1
  32.7 0.0 copy-done.7
  32.7 0.1 fusion.13
  32.8 0.0 copy-done.5
  32.8 0.0 copy-done.6
  32.8 0.3 fusion.44
  33.1 0.2 fusion.6
  33.3 0.0 copy-start.2
  33.3 0.0 copy-start.3
  33.3 0.3 convolution_convert_fusion.1
  33.7 0.0 copy-start.1
  33.7 0.1 fusion.35
  33.8 0.7 copy-done.2
  34.5 0.1 copy-done.3
  34.7 0.3 convolution_convert_fusion.2
  35.0 0.0 copy-start.4
  35.0 0.7 broadcast_in_dim.65
  35.7 15.0 %scatter_fusion.1 = bf16[128,2,256]{2,1,0:T(2,128)(2,1)} fusion(bf16[128,2,256]{2,1,0:T(2,128)(2,1)} %broadcast_in_dim.65, s32[128]{0:T(128)S(1)} %fusion.38, bf16[128,256]{1,0:T(8,128)(2,1)S(1)} %convolution_convert_fusion.2), kind=kCustom, calls=%fused_computation.2 | custom fusion | bytes 197632 | tf_op jit(solution)/shard_map/scatter | solution.py:76
  50.8 0.0 all-to-all-done
  50.8 13.6 %all-to-all-start.1 = ((bf16[128,2,256]{2,1,0:T(2,128)(2,1)}), bf16[128,2,256]{2,1,0:T(2,128)(2,1)S(1)}, u32[]{:S(2)}, u32[]{:S(2)}) async-start(bf16[128,2,256]{2,1,0:T(2,128)(2,1)} %scatter_fusion.1), calls=%async_computation.1 | async-start | bytes 262144 | tf_op jit(solution)/shard_map/all_to_all | solution.py:84
  64.4 0.0 reduce-scatter.2.cloned.1.call-start
  64.5 0.2 maximum_reduce_fusion
  64.7 0.1 reshape.410
  64.8 0.2 compare_reduce_fusion
  65.0 0.1 ge.44
  65.2 0.0 copy-done.1
  65.2 1.9 %gather_fusion = s32[256]{0:T(256)S(1)} fusion(s32[128]{0:T(128)S(1)} %bitcast.81, s32[1024]{0:T(1024)S(1)} %pad_clamp_fusion), kind=kCustom, calls=%fused_computation | custom fusion | bytes 3072 | tf_op jit(solution)/shard_map/gather | solution.py:89
  67.1 0.1 ge.42
  67.3 9.1 %all-to-all-done.1 = bf16[128,2,256]{2,1,0:T(2,128)(2,1)S(1)} async-done(((bf16[128,2,256]{2,1,0:T(2,128)(2,1)}), bf16[128,2,256]{2,1,0:T(2,128)(2,1)S(1)}, u32[]{:S(2)}, u32[]{:S(2)}) %all-to-all-start.1) | async-done | bytes 131104 | tf_op jit(solution)/shard_map/all_to_all | solution.py:84
  76.4 0.1 reshape.400
  76.5 0.1 copy.48
  76.6 0.3 fusion.24
  76.9 0.1 copy.40
  77.0 0.1 copy.41
  77.2 0.0 copy-done.4
  77.2 1.9 %scatter_custom_fusion.2 = bf16[1024,256]{1,0:T(8,128)(2,1)S(1)} fusion(bf16[1024,256]{1,0:T(8,128)(2,1)S(1)} %bitcast.86, s32[256]{0:T(256)S(1)} %bitcast.92, bf16[256,1,128]{2,0,1:T(8,128)(2,1)S(1)} %get-tuple-element.5, bf16[]{:T(256)} %constant.107, bf16[256,1,64]{2,0,1:T(8,128)(2,1)S(1)} %copy.41, bf16[256,1,64]{2,0,1:T(8,128)(2,1)S(1)} %copy.40), kind=kCustom, calls=%fused_computation.31 | custom fusion | flops 393216 | bytes 720898 | tf_op jit(solution)/shard_map/scatter | solution.py:110
  79.1 0.3 fusion.43
  79.3 0.2 fusion.31
  79.5 0.2 fusion.4
  79.7 0.2 copy.46
  79.9 0.0 copy-done
  80.0 1.7 %convolution_convert_fusion = bf16[258,2048]{1,0:T(8,128)(2,1)} fusion(bf16[512,2048]{1,0:T(8,128)(2,1)S(1)} %copy-done, bf16[2,512]{0,1:T(8,128)(2,1)S(1)} %bitcast.83, bf16[256,512]{0,1:T(8,128)(2,1)S(1)} %bitcast.87), kind=kOutput, calls=%fused_computation.4 | convolution fusion | flops 542121984 | bytes 3418112 | tf_op jit(solution)/shard_map/dot_general | solution.py:159
  81.7 0.0 reduce-scatter.2.cloned.1.call-update
  81.7 21.9 %reduce-scatter.2.cloned.1.call-done = bf16[258,512]{1,0:T(8,128)(2,1)} async-done(((bf16[258,2048]{1,0:T(8,128)(2,1)}), bf16[258,512]{1,0:T(8,128)(2,1)}) %reduce-scatter.2.cloned.1.call-update) | async-done | bytes 264208 | tf_op jit(solution)/shard_map/reduce_scatter | solution.py:160
  103.7 1.3 %slice.61 = bf16[2,512]{1,0:T(2,128)(2,1)} slice(bf16[258,512]{1,0:T(8,128)(2,1)} %reduce-scatter.2.cloned.1.call-done), slice={[256:258], [0:512]} | slice | bytes 4096 | tf_op jit(solution)/shard_map/slice | solution.py:163
  104.9 1.7 %slice.60 = bf16[256,512]{1,0:T(8,128)(2,1)} slice(bf16[258,512]{1,0:T(8,128)(2,1)} %reduce-scatter.2.cloned.1.call-done), slice={[0:256], [0:512]} | slice | bytes 524288 | tf_op jit(solution)/shard_map/slice | solution.py:163
  (12 shorter events, 0.1 us)
Async XLA Ops:
  7.2 72.8 %copy-start = (bf16[512,2048]{1,0:T(8,128)(2,1)S(1)}, bf16[512,2048]{1,0:T(8,128)(2,1)}, u32[]{:S(2)}) copy-start(bf16[512,2048]{1,0:T(8,128)(2,1)} %param.23) | copy-start | bytes 6291460
  7.2 25.6 %copy-start.5 = (bf16[256,512]{1,0:T(8,128)(2,1)S(1)}, bf16[256,512]{1,0:T(8,128)(2,1)}, u32[]{:S(2)}) copy-start(bf16[256,512]{1,0:T(8,128)(2,1)} %param.12) | copy-start | bytes 786436
  7.2 25.6 %copy-start.6 = (bf16[256,1,256]{2,0,1:T(8,128)(2,1)S(1)}, bf16[256,1,256]{2,0,1:T(8,128)(2,1)}, u32[]{:S(2)}) copy-start(bf16[256,1,256]{2,0,1:T(8,128)(2,1)} %param.13) | copy-start | bytes 393220
  7.2 25.5 %copy-start.7 = (s32[1,256]{1,0:T(1,128)S(1)}, s32[1,256]{1,0:T(1,128)}, u32[]{:S(2)}) copy-start(s32[1,256]{1,0:T(1,128)} %param.14) | copy-start | bytes 3076
  7.2 25.4 %copy-start.8 = (bf16[2,512]{1,0:T(2,128)(2,1)S(1)}, bf16[2,512]{1,0:T(2,128)(2,1)}, u32[]{:S(2)}) copy-start(bf16[2,512]{1,0:T(2,128)(2,1)} %param.15) | copy-start | bytes 6148
  7.2 25.3 %copy-start.9 = (bf16[2,1,256]{2,0,1:T(2,128)(2,1)S(1)}, bf16[2,1,256]{2,0,1:T(2,128)(2,1)}, u32[]{:S(2)}) copy-start(bf16[2,1,256]{2,0,1:T(2,128)(2,1)} %param.16) | copy-start | bytes 3076
  7.2 25.4 %copy-start.10 = (s32[2]{0:T(128)S(1)}, s32[2]{0:T(128)}, u32[]{:S(2)}) copy-start(s32[2]{0:T(128)} %param.18) | copy-start | bytes 28
  15.2 35.6 %all-to-all-start = ((s32[128,1,2]{2,1,0:T(1,128)}), s32[128,1,2]{2,1,0:T(1,128)S(1)}, u32[]{:S(2)}, u32[]{:S(2)}) async-start(s32[128,1,2]{2,1,0:T(1,128)} %copy.38), calls=%async_computation | async-start | bytes 131072 | tf_op jit(solution)/shard_map/all_to_all | solution.py:85
  33.3 1.2 %copy-start.2 = (bf16[2048,1,256]{2,0,1:T(8,128)(2,1)S(1)}, bf16[2048,1,256]{2,0,1:T(8,128)(2,1)}, u32[]{:S(2)}) copy-start(bf16[2048,1,256]{2,0,1:T(8,128)(2,1)} %param.22) | copy-start | bytes 3145732
  33.3 1.3 %copy-start.3 = (bf16[128,2048]{1,0:T(8,128)(2,1)S(1)}, bf16[128,2048]{1,0:T(8,128)(2,1)}, u32[]{:S(2)}) copy-start(bf16[128,2048]{1,0:T(8,128)(2,1)} %param.19) | copy-start | bytes 1572868
  33.7 31.5 %copy-start.1 = (s32[1,128]{1,0:T(1,128)S(1)}, s32[1,128]{1,0:T(1,128)}, u32[]{:S(2)}) copy-start(s32[1,128]{1,0:T(1,128)} %param.21) | copy-start | bytes 1540
  35.0 42.2 %copy-start.4 = (bf16[2,512,1,256]{3,1,2,0:T(8,128)(2,1)S(1)}, bf16[2,512,1,256]{3,1,2,0:T(8,128)(2,1)}, u32[]{:S(2)}) copy-start(bf16[2,512,1,256]{3,1,2,0:T(8,128)(2,1)} %param.17) | copy-start | bytes 1572868
  50.8 25.6 %all-to-all-start.1 = ((bf16[128,2,256]{2,1,0:T(2,128)(2,1)}), bf16[128,2,256]{2,1,0:T(2,128)(2,1)S(1)}, u32[]{:S(2)}, u32[]{:S(2)}) async-start(bf16[128,2,256]{2,1,0:T(2,128)(2,1)} %scatter_fusion.1), calls=%async_computation.1 | async-start | bytes 262144 | tf_op jit(solution)/shard_map/all_to_all | solution.py:84
  64.4 39.2 %reduce-scatter.2.cloned.1.call-start = ((), (), s32[]{:S(2)}) async-start(), calls=%async_computation.3 | async-start | bytes 1351680 | tf_op jit(solution)/shard_map/reduce_scatter | solution.py:160
Sparse Core Ops, SparseCore 0:
  81.8 21.7 reduce-scatter.1
where the time goes:
time: 114 us; the launch traced here: 113 us
  waiting for transfers between devices  31.1 us (27%)
  starting transfers between devices  31 us (27%)
  local copies, waits for them, and re-layouts  29.6 us (26%)
  between operations  14.4 us (13%)
  other arithmetic  4.03 us (4%)
  matrix products  3.3 us (3%)
    reduce_scatter x1, waiting for transfers between devices, shards(): lax.psum_scatter(partial_sums.astype(jnp.bfloat16), 'tp', scatter_dimensi...  21.9 us
    all_to_all x1, starting transfers between devices, shards(): lax.all_to_all(send_index, 'req', split_axis=0, concat_axis=0, tiled=True)  17.4 us
    scatter x1, local copies, waits for them, and re-layouts, shards(): send_rows = jnp.zeros((peer_count, CAP, rebuilt_rows.shape[1]), jnp.bfloa...  15 us
    all_to_all x1, starting transfers between devices, shards(): lax.all_to_all(send_rows, 'req', split_axis=0, concat_axis=0, tiled=True)  13.6 us
    all_to_all x1, waiting for transfers between devices, shards(): lax.all_to_all(send_rows, 'req', split_axis=0, concat_axis=0, tiled=True)  9.12 us
    scatter x1, local copies, waits for them, and re-layouts, shards(): send_index = jnp.full((peer_count, CAP), -1, jnp.int32).at[where_to, slot...  6.37 us
    slice x2, local copies, waits for them, and re-layouts, shards(): return (summed[:prompt_rows], summed[prompt_rows:])  2.95 us
  transfers between devices with their start and end apart: 3, of which 2 were waited for; matrix products, arithmetic and copies ran while one was open for 18% of the time, Pallas kernels for 0%

commit v1 on v0

v1 whole, which is shorter than its diff:
```python
import jax
import jax.numpy as jnp
import numpy as np
from jax import lax
from jax.experimental import pallas as pl
from jax.experimental.pallas import tpu as pltpu
from jax.sharding import PartitionSpec as P

CAP = 2
ROPE_BASE = 600000.0
F32 = jnp.float32
BF16 = jnp.bfloat16


def dot(a, b, ca, cb):
    return lax.dot_general(a, b, (((ca,), (cb,)), ((), ())), preferred_element_type=F32)


def call(kernel, outs, *args, scalars=()):
    vmem = pl.BlockSpec(memory_space=pltpu.VMEM)
    smem = pl.BlockSpec(memory_space=pltpu.SMEM)
    return pl.pallas_call(
        kernel,
        out_shape=outs,
        in_specs=[smem] * len(scalars) + [vmem] * len(args),
        out_specs=jax.tree.map(lambda _: vmem, outs),
    )(*scalars, *args)


def pack_kernel(hidden, weight, dest, out):
    peers, cap, width = out.shape
    rows = hidden.shape[0]
    rebuilt = dot(hidden[...], weight[...], 1, 0).astype(BF16)
    number = lax.broadcasted_iota(jnp.int32, (1, rows), 1)
    code = dest[...] * cap + number % cap
    code = jnp.where(dest[...] >= 0, code, -1)
    place = lax.broadcasted_iota(jnp.int32, (peers * cap, rows), 0)
    chosen = jnp.where(place == code, 1.0, 0.0).astype(BF16)
    packed = dot(chosen, rebuilt, 1, 0).astype(BF16)
    both = jnp.concatenate([packed, chosen], axis=1)
    out[...] = both.reshape(peers, cap, width)


def prompt_kernel(query, key_value, segment, weight, out):
    tokens, _ = query.shape
    head = key_value.shape[1] // 2
    groups = query.shape[1] // head
    parts, _, share = out.shape
    scale = head**-0.5
    same = jnp.where(
        lax.broadcasted_iota(jnp.int32, (8, tokens), 0) == segment[...], 1.0, 0.0
    ).astype(BF16)
    same = dot(same, same, 0, 0)
    row = lax.broadcasted_iota(jnp.int32, (tokens, tokens), 0)
    col = lax.broadcasted_iota(jnp.int32, (tokens, tokens), 1)
    allowed = (same > 0.5) & (col <= row)
    keys = key_value[:, :head]
    values = key_value[:, head:]
    mixed = []
    for g in range(groups):
        scores = dot(query[:, g * head : (g + 1) * head], keys, 1, 1) * scale
        scores = jnp.where(allowed, scores, -jnp.inf)
        power = jnp.exp(scores - jnp.max(scores, axis=1, keepdims=True))
        total = jnp.sum(power, axis=1, keepdims=True)
        mix = dot(power.astype(BF16), values, 1, 0)
        mixed.append((mix / total).astype(BF16))
    mixed = jnp.concatenate(mixed, axis=1)
    for t in range(parts):
        out[t] = dot(mixed, weight[:, t * share : (t + 1) * share], 1, 0).astype(BF16)


def queries_by_row(query, head):
    wide = query[...].astype(F32)
    groups = wide.shape[1] // head
    return jnp.concatenate(
        [wide[:, g * head : (g + 1) * head] for g in range(groups)], axis=0
    ).astype(BF16)


def before_kernel(length, query, own, cache, slots, frequency, top_o, total_o, mix_o, cos_o, sin_o):
    head = cache.shape[1] // 2
    decoders = query.shape[0]
    cache_len = cache.shape[0] // decoders
    scale = head**-0.5
    q = queries_by_row(query, head)
    rows = q.shape[0]
    listed = slots.shape[1]
    slot_col = jnp.broadcast_to(slots[...].astype(F32), (listed, listed)).T
    place = lax.broadcasted_iota(jnp.int32, (1, cache.shape[0]), 1).astype(F32)
    hit = jnp.max(jnp.where(slot_col[:, :1] == place, 1.0, 0.0), axis=0, keepdims=True)
    row = lax.broadcasted_iota(jnp.int32, (rows, cache.shape[0]), 0)
    col = lax.broadcasted_iota(jnp.int32, (rows, cache.shape[0]), 1)
    decoder = row % decoders
    offset = col - decoder * cache_len
    limit = jnp.full_like(row, length[0])
    for b in range(1, decoders):
        limit = jnp.where(decoder == b, length[b], limit)
    live = (offset >= 0) & (offset < limit) & (offset < cache_len) & (hit < 0.5)
    scores = dot(q, cache[:, :head], 1, 1) * scale
    scores = jnp.where(live, scores, -jnp.inf)
    pair = own[...].astype(F32)
    pair = jnp.concatenate([pair] * (rows // decoders), axis=0)
    self_score = jnp.sum(q.astype(F32) * pair[:, :head], axis=1, keepdims=True) * scale
    top = jnp.maximum(jnp.max(scores, axis=1, keepdims=True), self_score)
    power = jnp.exp(scores - top)
    own_power = jnp.exp(self_score - top)
    total = own_power + jnp.sum(power, axis=1, keepdims=True)
    mix = dot(power.astype(BF16), cache[:, head:], 1, 0)
    mix = mix + own_power.astype(BF16).astype(F32) * pair[:, head:]
    top_o[...] = jnp.broadcast_to(top, top_o.shape)
    total_o[...] = jnp.broadcast_to(total, total_o.shape)
    mix_o[...] = mix
    position = jnp.maximum(slot_col, 0.0)
    position = position - cache_len * jnp.floor(position * (1.0 / cache_len))
    angle = position * frequency[...]
    lane = lax.broadcasted_iota(jnp.int32, angle.shape, 1)
    cos_o[...] = jnp.cos(angle)
    sine = jnp.sin(angle)
    sin_o[...] = jnp.where(lane < head // 2, -sine, sine)


def after_kernel(length, got, query, slots, top_i, total_i, mix_i, cos_i, sin_i, weight, out):
    peers, cap, width = got.shape
    listed = slots.shape[1]
    head = mix_i.shape[1]
    decoders = query.shape[0]
    parts, _, share = out.shape
    cache_len = 512
    scale = head**-0.5
    flat = got[...].reshape(peers * cap, width)
    ordered = dot(flat[:, 2 * head :], flat[:, : 2 * head], 0, 0)
    key = ordered[:, :head]
    value = ordered[:, head:].astype(BF16)
    turned = (key * cos_i[...] + pltpu.roll(key, head // 2, 1) * sin_i[...]).astype(BF16)
    q = queries_by_row(query, head)
    rows = q.shape[0]
    scores = dot(q, turned, 1, 1) * scale
    row = lax.broadcasted_iota(jnp.int32, (rows, listed), 0)
    decoder = row % decoders
    limit = jnp.full_like(row, length[0])
    for b in range(1, decoders):
        limit = jnp.where(decoder == b, length[b], limit)
    offset = slots[...] - decoder * cache_len
    live = (slots[...] >= 0) & (offset >= 0) & (offset < limit) & (offset < cache_len)
    scores = jnp.where(live, scores, -jnp.inf)
    top = jnp.maximum(top_i[...], jnp.max(scores, axis=1, keepdims=True))
    power = jnp.exp(scores - top)
    keep = jnp.exp(top_i[...] - top)
    total = keep * total_i[...] + jnp.sum(power, axis=1, keepdims=True)
    mix = keep * mix_i[...] + dot(power.astype(BF16), value, 1, 0)
    mix = mix / total
    mixed = jnp.concatenate(
        [mix[i : i + decoders] for i in range(0, rows, decoders)], axis=1
    ).astype(BF16)
    for t in range(parts):
        out[t] = dot(mixed, weight[:, t * share : (t + 1) * share], 1, 0).astype(BF16)


def shards(
    prompt_query,
    prompt_key_value,
    prompt_segment_index,
    decoder_query,
    decoder_key_value,
    key_value_cache,
    live_cache_length,
    rebuild_hidden_state,
    owner_dest,
    miss_pos,
    key_value_weight,
    out_weight,
):
    pair = prompt_key_value.shape[-1]
    head = pair // 2
    peers = lax.axis_size("req")
    parts = lax.axis_size("tp")
    decoders = key_value_cache.shape[0]
    tokens = prompt_query.shape[0]
    listed = rebuild_hidden_state.shape[0]
    share = out_weight.shape[1] // parts
    shape = jax.ShapeDtypeStruct

    send = call(
        pack_kernel,
        shape((peers, CAP, pair + listed), BF16),
        rebuild_hidden_state,
        key_value_weight.reshape(-1, pair),
        owner_dest,
    )
    got = lax.all_to_all(send, "req", split_axis=0, concat_axis=0, tiled=True)

    prompt_part = call(
        prompt_kernel,
        shape((parts, tokens, share), BF16),
        prompt_query,
        prompt_key_value.reshape(tokens, pair),
        prompt_segment_index,
        out_weight,
    )
    half = head // 2
    frequency = (ROPE_BASE ** (-2.0 * (np.arange(head) % half) / head)).astype(np.float32)
    rows = decoder_query.shape[1] // head * decoders
    state = call(
        before_kernel,
        [shape((rows, head), F32)] * 3 + [shape((listed, head), F32)] * 2,
        decoder_query,
        decoder_key_value.reshape(decoders, pair),
        key_value_cache.reshape(-1, pair),
        miss_pos,
        jnp.asarray(frequency).reshape(1, head),
        scalars=(live_cache_length,),
    )
    prompt_got = lax.all_to_all(prompt_part, "tp", split_axis=0, concat_axis=0, tiled=True)
    dec_part = call(
        after_kernel,
        shape((parts, decoders, share), BF16),
        got,
        decoder_query,
        miss_pos,
        *state,
        out_weight,
        scalars=(live_cache_length,),
    )
    dec_got = lax.all_to_all(dec_part, "tp", split_axis=0, concat_axis=0, tiled=True)
    prompt_out = jnp.sum(prompt_got.astype(F32), axis=0).astype(BF16)
    dec_out = jnp.sum(dec_got.astype(F32), axis=0).astype(BF16)
    return prompt_out, dec_out


def solution(mesh):
    in_specs = (
        P("req", "tp"),
        P("req", "tp", None),
        P("req", None),
        P("req", "tp"),
        P("req", "tp", None),
        P("req", None, "tp", None),
        P("req"),
        P("req", None),
        P("req", None),
        P("req", None),
        P(None, "tp", None),
        P("tp", None),
    )
    out_specs = (P("req", "tp"), P("req", "tp"))
    return jax.shard_map(shards, mesh=mesh, in_specs=in_specs, out_specs=out_specs, check_vma=False)
```

time: 114 us -> 67.1 us (0.59)
  local copies, waits for them, and re-layouts: 29.6 us -> 0.68 us
  between operations: 14.4 us -> 0.65 us
  Pallas kernels: 0 us -> 12.3 us
  starting transfers between devices: 31 us -> 25.2 us
  waiting for transfers between devices: 31.1 us -> 26.4 us
  matrix products: 3.3 us -> 0 us
  other arithmetic: 4.03 us -> 1.5 us
    reduce_scatter x1 -> x0, waiting for transfers between devices: 21.9 us -> none  [shards(): lax.psum_scatter(partial_sums.astype(jnp.bfloat16), 'tp', scatter_dimensi...]
    scatter x2 -> x0, local copies, waits for them, and re-layouts: 21.4 us -> none  [the longest x1 15 us: shards(): send_rows = jnp.zeros((peer_count, CAP, rebuilt_rows.shape[1]), jnp.bfloa...]
    all_to_all x2 -> x3, waiting for transfers between devices: 9.12 us -> 26.4 us  [the longest x1 14 us: shards(): lax.all_to_all(prompt_part, 'tp', split_axis=0, concat_axis=0, tiled=True)]
    pallas_call x0 -> x4, Pallas kernels: none -> 12.3 us  [call(): pl.pallas_call(kernel, out_shape=outs, in_specs=[smem] * len(scalars) + [...]
    all_to_all x2 -> x3, starting transfers between devices: 31 us -> 25.2 us  [the longest x1 17.4 us: shards(): got = lax.all_to_all(send, 'req', split_axis=0, concat_axis=0, tiled=True)]
    dot_general x7 -> x0, matrix products: 3.3 us -> none  [the longest x1 1.74 us: shards(): jnp.dot(combined, out_weight, preferred_element_type=jnp.float32)]
    slice x3 -> x0, local copies, waits for them, and re-layouts: 2.96 us -> none  [the longest x2 2.95 us: shards(): return (summed[:prompt_rows], summed[prompt_rows:])]
    scatter x1 -> x0, other arithmetic: 1.9 us -> none  [shards(): updated_cache = key_value_cache.reshape(total_slots, local_heads, 2 * hea...]
  transfers between devices with their start and end apart: 3 -> 3, of which waited for: 2 -> 3; matrix products, arithmetic and copies ran while one was open for 18% -> 1% of each run, Pallas kernels for 0% -> 9%
where the time goes in v1:
time: 67.1 us; the launch traced here: 66.6 us
  waiting for transfers between devices  26.4 us (39%)
  starting transfers between devices  25.2 us (38%)
  Pallas kernels  12.3 us (18%)
  other arithmetic  1.5 us (2%)
  local copies, waits for them, and re-layouts  0.68 us (1%)
    all_to_all x1, starting transfers between devices, shards(): got = lax.all_to_all(send, 'req', split_axis=0, concat_axis=0, tiled=True)  17.4 us
    all_to_all x1, waiting for transfers between devices, shards(): lax.all_to_all(prompt_part, 'tp', split_axis=0, concat_axis=0, tiled=True)  14 us
    pallas_call x4, Pallas kernels, call(): pl.pallas_call(kernel, out_shape=outs, in_specs=[smem] * len(scalars) + [...  12.3 us
    all_to_all x1, waiting for transfers between devices, shards(): got = lax.all_to_all(send, 'req', split_axis=0, concat_axis=0, tiled=True)  11 us
    all_to_all x1, starting transfers between devices, shards(): lax.all_to_all(dec_part, 'tp', split_axis=0, concat_axis=0, tiled=True)  4.29 us
    all_to_all x1, starting transfers between devices, shards(): lax.all_to_all(prompt_part, 'tp', split_axis=0, concat_axis=0, tiled=True)  3.52 us
  transfers between devices with their start and end apart: 3, of which 3 were waited for; matrix products, arithmetic and copies ran while one was open for 1% of the time, Pallas kernels for 9%

profile of v1, /device:TPU:8, one launch (start us, length us, event | category | flops | bytes accessed | tf_op | source)
XLA Modules:
  0.0 66.6 jit_solution(17570464352451353501)
XLA Ops:
  0.6 2.6 %shard_map.141 = bf16[128,2,384]{2,1,0:T(2,128)(2,1)} custom-call(bf16[128,2048]{1,0:T(8,128)(2,1)} %hidden.1, bf16[2048,256]{1,0:T(8,128)(2,1)} %bitcast.4, s32[1,128]{1,0:T(1,128)} %dest.1), custom_call_target="tpu_custom_call" | custom-call | tf_op jit(solution)/shard_map/pallas_call | solution.py:22
  3.2 17.4 %all-to-all-start.1 = ((bf16[128,2,384]{2,1,0:T(2,128)(2,1)}), bf16[128,2,384]{2,1,0:T(2,128)(2,1)S(1)}, u32[]{:S(2)}, u32[]{:S(2)}) async-start(bf16[128,2,384]{2,1,0:T(2,128)(2,1)} %shard_map.141), calls=%async_computation.1 | async-start | bytes 393216 | tf_op jit(solution)/shard_map/all_to_all | solution.py:190
  20.6 2.3 %shard_map.142 = (f32[8,128]{1,0:T(8,128)}, f32[8,128]{1,0:T(8,128)}, f32[8,128]{1,0:T(8,128)}, f32[128,128]{1,0:T(8,128)}, f32[128,128]{1,0:T(8,128)}) custom-call(s32[2]{0:T(128)} %length.3, bf16[2,512]{1,0:T(2,128)(2,1)} %query.5, bf16[2,256]{1,0:T(2,128)(2,1)} %bitcast.7, bf16[1024,256]{1,0:T(8,128)(2,1)} %bitcast.5, s32[1,128]{1,0:T(1,128)} %slots.3, ...), custom_call_target="tpu_custom_call" | custom-call | tf_op jit(solution)/shard_map/pallas_call | solution.py:22
  22.9 11.0 %all-to-all-done.1.got = bf16[128,2,384]{2,1,0:T(2,128)(2,1)S(1)} async-done(((bf16[128,2,384]{2,1,0:T(2,128)(2,1)}), bf16[128,2,384]{2,1,0:T(2,128)(2,1)S(1)}, u32[]{:S(2)}, u32[]{:S(2)}) %all-to-all-start.1) | async-done | bytes 196640 | tf_op jit(solution)/shard_map/all_to_all | solution.py:190
  33.9 0.0 copy-start
  33.9 0.7 %copy-done = bf16[128,2,384]{2,1,0:T(2,128)(2,1)} copy-done((bf16[128,2,384]{2,1,0:T(2,128)(2,1)}, bf16[128,2,384]{2,1,0:T(2,128)(2,1)S(1)}, u32[]{:S(2)}) %copy-start) | copy-done | bytes 196632
  34.5 3.4 %shard_map.143 = bf16[4,2,512]{2,1,0:T(2,128)(2,1)} custom-call(s32[2]{0:T(128)} %length.3, bf16[128,2,384]{2,1,0:T(2,128)(2,1)} %copy-done, bf16[2,512]{1,0:T(2,128)(2,1)} %query.5, s32[1,128]{1,0:T(1,128)} %slots.3, f32[8,128]{1,0:T(8,128)} %get-tuple-element.7.top_i, f32[8,128]{1,0:T(8,128)} %get-tuple-element.8.total_i, ...), custom_call_target="tpu_custom_call" | custom-call | tf_op jit(solution)/shard_map/pallas_call | solution.py:22
  37.9 4.3 %all-to-all-start.2 = ((bf16[4,2,512]{2,1,0:T(2,128)(2,1)}), bf16[4,2,512]{2,1,0:T(2,128)(2,1)S(1)}, u32[]{:S(2)}, u32[]{:S(2)}) async-start(bf16[4,2,512]{2,1,0:T(2,128)(2,1)} %shard_map.143), calls=%async_computation.2 | async-start | bytes 16384 | tf_op jit(solution)/shard_map/all_to_all | solution.py:224
  42.2 4.0 %shard_map.140 = bf16[4,256,512]{2,1,0:T(8,128)(2,1)} custom-call(bf16[256,512]{1,0:T(8,128)(2,1)} %query.3, bf16[256,256]{1,0:T(8,128)(2,1)} %bitcast.6, s32[1,256]{1,0:T(1,128)} %segment.1, bf16[512,2048]{1,0:T(8,128)(2,1)} %weight.3), custom_call_target="tpu_custom_call" | custom-call | tf_op jit(solution)/shard_map/pallas_call | solution.py:22
  46.2 1.3 %all-to-all-done.2 = bf16[4,2,512]{2,1,0:T(2,128)(2,1)S(1)} async-done(((bf16[4,2,512]{2,1,0:T(2,128)(2,1)}), bf16[4,2,512]{2,1,0:T(2,128)(2,1)S(1)}, u32[]{:S(2)}, u32[]{:S(2)}) %all-to-all-start.2) | async-done | bytes 8224 | tf_op jit(solution)/shard_map/all_to_all | solution.py:224
  47.5 3.5 %all-to-all-start = ((bf16[4,256,512]{2,1,0:T(8,128)(2,1)}), bf16[4,256,512]{2,1,0:T(8,128)(2,1)S(1)}, u32[]{:S(2)}, u32[]{:S(2)}) async-start(bf16[4,256,512]{2,1,0:T(8,128)(2,1)} %shard_map.140), calls=%async_computation | async-start | bytes 2097152 | tf_op jit(solution)/shard_map/all_to_all | solution.py:213
  51.1 0.6 reduce_sum.25
  51.7 14.0 %all-to-all-done = bf16[4,256,512]{2,1,0:T(8,128)(2,1)S(1)} async-done(((bf16[4,256,512]{2,1,0:T(8,128)(2,1)}), bf16[4,256,512]{2,1,0:T(8,128)(2,1)S(1)}, u32[]{:S(2)}, u32[]{:S(2)}) %all-to-all-start) | async-done | bytes 1048608 | tf_op jit(solution)/shard_map/all_to_all | solution.py:213
  65.7 0.9 %reduce_sum.24 = bf16[256,512]{1,0:T(8,128)(2,1)} reduce(bf16[4,256,512]{2,1,0:T(8,128)(2,1)S(1)} %all-to-all-done, bf16[]{:T(256)} %constant.5.clone.1), dimensions={0}, to_apply=%region_0.0 | reduce | flops 393216 | bytes 1310722 | tf_op jit(solution)/shard_map/reduce_sum | solution.py:225
Async XLA Ops:
  3.2 30.7 %all-to-all-start.1 = ((bf16[128,2,384]{2,1,0:T(2,128)(2,1)}), bf16[128,2,384]{2,1,0:T(2,128)(2,1)S(1)}, u32[]{:S(2)}, u32[]{:S(2)}) async-start(bf16[128,2,384]{2,1,0:T(2,128)(2,1)} %shard_map.141), calls=%async_computation.1 | async-start | bytes 393216 | tf_op jit(solution)/shard_map/all_to_all | solution.py:190
  33.9 0.7 %copy-start = (bf16[128,2,384]{2,1,0:T(2,128)(2,1)}, bf16[128,2,384]{2,1,0:T(2,128)(2,1)S(1)}, u32[]{:S(2)}) copy-start(bf16[128,2,384]{2,1,0:T(2,128)(2,1)S(1)} %all-to-all-done.1.got) | copy-start | bytes 589828
  37.9 9.6 %all-to-all-start.2 = ((bf16[4,2,512]{2,1,0:T(2,128)(2,1)}), bf16[4,2,512]{2,1,0:T(2,128)(2,1)S(1)}, u32[]{:S(2)}, u32[]{:S(2)}) async-start(bf16[4,2,512]{2,1,0:T(2,128)(2,1)} %shard_map.143), calls=%async_computation.2 | async-start | bytes 16384 | tf_op jit(solution)/shard_map/all_to_all | solution.py:224
  47.5 18.2 %all-to-all-start = ((bf16[4,256,512]{2,1,0:T(8,128)(2,1)}), bf16[4,256,512]{2,1,0:T(8,128)(2,1)S(1)}, u32[]{:S(2)}, u32[]{:S(2)}) async-start(bf16[4,256,512]{2,1,0:T(8,128)(2,1)} %shard_map.140), calls=%async_computation | async-start | bytes 2097152 | tf_op jit(solution)/shard_map/all_to_all | solution.py:213

commit v2 on v1

--- a/solution.py
+++ b/solution.py
@@ -41,11 +41,11 @@
     out[...] = both.reshape(peers, cap, width)
 
 
-def prompt_kernel(query, key_value, segment, weight, out):
+def prompt_kernel(place, query, key_value, segment, weight, *outs):
     tokens, _ = query.shape
     head = key_value.shape[1] // 2
     groups = query.shape[1] // head
-    parts, _, share = out.shape
+    parts, share = len(outs), outs[0].shape[1]
     scale = head**-0.5
     same = jnp.where(
         lax.broadcasted_iota(jnp.int32, (8, tokens), 0) == segment[...], 1.0, 0.0
@@ -65,8 +65,10 @@
         mix = dot(power.astype(BF16), values, 1, 0)
         mixed.append((mix / total).astype(BF16))
     mixed = jnp.concatenate(mixed, axis=1)
-    for t in range(parts):
-        out[t] = dot(mixed, weight[:, t * share : (t + 1) * share], 1, 0).astype(BF16)
+    for k in range(parts):
+        to = lax.rem(place[0] + k, parts)
+        columns = pl.ds(pl.multiple_of(to * share, share), share)
+        outs[k][...] = dot(mixed, weight[:, columns], 1, 0).astype(BF16)
 
 
 def queries_by_row(query, head):
@@ -191,12 +193,17 @@
 
     prompt_part = call(
         prompt_kernel,
-        shape((parts, tokens, share), BF16),
+        [shape((tokens, share), BF16)] * parts,
         prompt_query,
         prompt_key_value.reshape(tokens, pair),
         prompt_segment_index,
         out_weight,
-    )
+        scalars=(lax.axis_index("tp").reshape(1),),
+    )
+    arrived = [
+        lax.ppermute(prompt_part[k], "tp", [(i, (i + k) % parts) for i in range(parts)])
+        for k in range(1, parts)
+    ]
     half = head // 2
     frequency = (ROPE_BASE ** (-2.0 * (np.arange(head) % half) / head)).astype(np.float32)
     rows = decoder_query.shape[1] // head * decoders
@@ -210,7 +217,6 @@
         jnp.asarray(frequency).reshape(1, head),
         scalars=(live_cache_length,),
     )
-    prompt_got = lax.all_to_all(prompt_part, "tp", split_axis=0, concat_axis=0, tiled=True)
     dec_part = call(
         after_kernel,
         shape((parts, decoders, share), BF16),
@@ -222,8 +228,11 @@
         scalars=(live_cache_length,),
     )
     dec_got = lax.all_to_all(dec_part, "tp", split_axis=0, concat_axis=0, tiled=True)
-    prompt_out = jnp.sum(prompt_got.astype(F32), axis=0).astype(BF16)
     dec_out = jnp.sum(dec_got.astype(F32), axis=0).astype(BF16)
+    prompt_out = prompt_part[0].astype(F32)
+    for part in arrived:
+        prompt_out = prompt_out + part.astype(F32)
+    prompt_out = prompt_out.astype(BF16)
     return prompt_out, dec_out
 
 

time: 67.1 us -> 51 us (0.76)
  waiting for transfers between devices: 26.4 us -> 4.48 us
  starting transfers between devices: 25.2 us -> 31.3 us
    all_to_all x1 -> x0, waiting for transfers between devices: 14 us -> none  [shards(): lax.all_to_all(prompt_part, 'tp', split_axis=0, concat_axis=0, tiled=True)]
    all_to_all x1, waiting for transfers between devices: 11 us -> 0.01 us  [shards(): got = lax.all_to_all(send, 'req', split_axis=0, concat_axis=0, tiled=True)]
    ppermute x0 -> x3, starting transfers between devices: none -> 10.3 us  [shards(): lax.ppermute(prompt_part[k], 'tp', [(i, (i + k) % parts) for i in range(p...]
    all_to_all x1 -> x0, starting transfers between devices: 3.52 us -> none  [shards(): lax.all_to_all(prompt_part, 'tp', split_axis=0, concat_axis=0, tiled=True)]
    ppermute x0 -> x3, waiting for transfers between devices: none -> 1.77 us  [shards(): lax.ppermute(prompt_part[k], 'tp', [(i, (i + k) % parts) for i in range(p...]
    all_to_all x1, waiting for transfers between devices: 1.33 us -> 2.7 us  [shards(): lax.all_to_all(dec_part, 'tp', split_axis=0, concat_axis=0, tiled=True)]
    reduce_sum x1 -> x0, other arithmetic: 0.9 us -> none  [shards(): prompt_out = jnp.sum(prompt_got.astype(F32), axis=0).astype(BF16)]
    convert_element_type x0 -> x1, other arithmetic: none -> 0.84 us  [shards(): prompt_out = prompt_out.astype(BF16)]
  transfers between devices with their start and end apart: 3 -> 5, of which waited for: 3 -> 2; matrix products, arithmetic and copies ran while one was open for 1% -> 2% of each run, Pallas kernels for 9% -> 19%
where the time goes in v2:
time: 51 us; the launch traced here: 50.6 us
  starting transfers between devices  31.3 us (61%)
  Pallas kernels  12 us (24%)
  waiting for transfers between devices  4.48 us (9%)
  other arithmetic  1.43 us (3%)
  local copies, waits for them, and re-layouts  0.68 us (1%)
  between operations  0.68 us (1%)
    all_to_all x1, starting transfers between devices, shards(): got = lax.all_to_all(send, 'req', split_axis=0, concat_axis=0, tiled=True)  17.4 us
    pallas_call x4, Pallas kernels, call(): pl.pallas_call(kernel, out_shape=outs, in_specs=[smem] * len(scalars) + [...  12 us
    ppermute x3, starting transfers between devices, shards(): lax.ppermute(prompt_part[k], 'tp', [(i, (i + k) % parts) for i in range(p...  10.3 us
    all_to_all x1, starting transfers between devices, shards(): lax.all_to_all(dec_part, 'tp', split_axis=0, concat_axis=0, tiled=True)  3.63 us
    all_to_all x1, waiting for transfers between devices, shards(): lax.all_to_all(dec_part, 'tp', split_axis=0, concat_axis=0, tiled=True)  2.7 us
    ppermute x3, waiting for transfers between devices, shards(): lax.ppermute(prompt_part[k], 'tp', [(i, (i + k) % parts) for i in range(p...  1.77 us
  transfers between devices with their start and end apart: 5, of which 2 were waited for; matrix products, arithmetic and copies ran while one was open for 2% of the time, Pallas kernels for 19%

profile of v2, /device:TPU:8, one launch (start us, length us, event | category | flops | bytes accessed | tf_op | source)
XLA Modules:
  0.0 50.6 jit_solution(18416231078267070297)
XLA Ops:
  0.6 2.6 %shard_map.141 = bf16[128,2,384]{2,1,0:T(2,128)(2,1)} custom-call(bf16[128,2048]{1,0:T(8,128)(2,1)} %hidden.1, bf16[2048,256]{1,0:T(8,128)(2,1)} %bitcast.5, s32[1,128]{1,0:T(1,128)} %dest.1), custom_call_target="tpu_custom_call" | custom-call | tf_op jit(solution)/shard_map/pallas_call | solution.py:22
  3.2 17.4 %all-to-all-start = ((bf16[128,2,384]{2,1,0:T(2,128)(2,1)}), bf16[128,2,384]{2,1,0:T(2,128)(2,1)S(1)}, u32[]{:S(2)}, u32[]{:S(2)}) async-start(bf16[128,2,384]{2,1,0:T(2,128)(2,1)} %shard_map.141), calls=%async_computation | async-start | bytes 393216 | tf_op jit(solution)/shard_map/all_to_all | solution.py:192
  20.6 3.7 %shard_map.140 = (bf16[256,512]{1,0:T(8,128)(2,1)}, bf16[256,512]{1,0:T(8,128)(2,1)}, bf16[256,512]{1,0:T(8,128)(2,1)}, bf16[256,512]{1,0:T(8,128)(2,1)}) custom-call(s32[1]{0:T(128)} %bitcast.place, bf16[256,512]{1,0:T(8,128)(2,1)} %query.3, bf16[256,256]{1,0:T(8,128)(2,1)} %bitcast.7, s32[1,256]{1,0:T(1,128)} %segment.1, bf16[512,2048]{1,0:T(8,128)(2,1)} %weight.3), custom_call_target="tpu_custom_call" | custom-call | tf_op jit(solution)/shard_map/pallas_call | solution.py:22
  24.3 0.0 copy-start.1
  24.3 4.8 %collective-permute-start.2 = (bf16[256,512]{1,0:T(8,128)(2,1)}, bf16[256,512]{1,0:T(8,128)(2,1)S(1)}, u32[]{:S(2)}, u32[]{:S(2)}) collective-permute-start(bf16[256,512]{1,0:T(8,128)(2,1)} %get-tuple-element.14), channel_id=1, source_target_pairs={{0,3},{1,0},{2,1},{3,2},{4,7},{5,4},{6,5},{7,6},{8,11},{9,8},{10,9... | collective-permute-start | bytes 786440 | tf_op jit(solution)/shard_map/ppermute | solution.py:204
  29.1 2.7 %collective-permute-start.1 = (bf16[256,512]{1,0:T(8,128)(2,1)}, bf16[256,512]{1,0:T(8,128)(2,1)S(1)}, u32[]{:S(2)}, u32[]{:S(2)}) collective-permute-start(bf16[256,512]{1,0:T(8,128)(2,1)} %get-tuple-element.13), channel_id=1, source_target_pairs={{0,2},{1,3},{2,0},{3,1},{4,6},{5,7},{6,4},{7,5},{8,10},{9,11},{10,... | collective-permute-start | bytes 786440 | tf_op jit(solution)/shard_map/ppermute | solution.py:204
  31.8 2.8 %collective-permute-start = (bf16[256,512]{1,0:T(8,128)(2,1)}, bf16[256,512]{1,0:T(8,128)(2,1)S(1)}, u32[]{:S(2)}, u32[]{:S(2)}) collective-permute-start(bf16[256,512]{1,0:T(8,128)(2,1)} %get-tuple-element.12), channel_id=1, source_target_pairs={{0,1},{1,2},{2,3},{3,0},{4,5},{5,6},{6,7},{7,4},{8,9},{9,10},{10,1... | collective-permute-start | bytes 786440 | tf_op jit(solution)/shard_map/ppermute | solution.py:204
  34.6 2.3 %shard_map.142 = (f32[8,128]{1,0:T(8,128)}, f32[8,128]{1,0:T(8,128)}, f32[8,128]{1,0:T(8,128)}, f32[128,128]{1,0:T(8,128)}, f32[128,128]{1,0:T(8,128)}) custom-call(s32[2]{0:T(128)} %length.3, bf16[2,512]{1,0:T(2,128)(2,1)} %query.5, bf16[2,256]{1,0:T(2,128)(2,1)} %bitcast.8, bf16[1024,256]{1,0:T(8,128)(2,1)} %bitcast.6, s32[1,128]{1,0:T(1,128)} %slots.3, ...), custom_call_target="tpu_custom_call" | custom-call | tf_op jit(solution)/shard_map/pallas_call | solution.py:22
  36.9 0.0 all-to-all-done.got
  36.9 0.0 copy-start
  37.0 0.7 %copy-done = bf16[128,2,384]{2,1,0:T(2,128)(2,1)} copy-done((bf16[128,2,384]{2,1,0:T(2,128)(2,1)}, bf16[128,2,384]{2,1,0:T(2,128)(2,1)S(1)}, u32[]{:S(2)}) %copy-start) | copy-done | bytes 196632
  37.6 3.4 %shard_map.143 = bf16[4,2,512]{2,1,0:T(2,128)(2,1)} custom-call(s32[2]{0:T(128)} %length.3, bf16[128,2,384]{2,1,0:T(2,128)(2,1)} %copy-done, bf16[2,512]{1,0:T(2,128)(2,1)} %query.5, s32[1,128]{1,0:T(1,128)} %slots.3, f32[8,128]{1,0:T(8,128)} %get-tuple-element.15.top_i, f32[8,128]{1,0:T(8,128)} %get-tuple-element.16.total_i, ...), custom_call_target="tpu_custom_call" | custom-call | tf_op jit(solution)/shard_map/pallas_call | solution.py:22
  41.0 3.6 %all-to-all-start.1 = ((bf16[4,2,512]{2,1,0:T(2,128)(2,1)}), bf16[4,2,512]{2,1,0:T(2,128)(2,1)S(1)}, u32[]{:S(2)}, u32[]{:S(2)}) async-start(bf16[4,2,512]{2,1,0:T(2,128)(2,1)} %shard_map.143), calls=%async_computation.1 | async-start | bytes 16384 | tf_op jit(solution)/shard_map/all_to_all | solution.py:230
  44.6 0.0 collective-permute-done.2
  44.7 0.0 collective-permute-done.1
  44.7 1.8 %collective-permute-done = bf16[256,512]{1,0:T(8,128)(2,1)S(1)} collective-permute-done((bf16[256,512]{1,0:T(8,128)(2,1)}, bf16[256,512]{1,0:T(8,128)(2,1)S(1)}, u32[]{:S(2)}, u32[]{:S(2)}) %collective-permute-start) | collective-permute-done | bytes 262176 | tf_op jit(solution)/shard_map/ppermute | solution.py:204
  46.4 0.0 copy-done.1
  46.4 0.8 %add_convert_fusion = bf16[256,512]{1,0:T(8,128)(2,1)} fusion(bf16[256,512]{1,0:T(8,128)(2,1)S(1)} %collective-permute-done.2, bf16[256,512]{1,0:T(8,128)(2,1)S(1)} %collective-permute-done.1, bf16[256,512]{1,0:T(8,128)(2,1)S(1)} %collective-permute-done, bf16[256,512]{1,0:T(8,128)(2,1)S(1)} %copy-done.1), kind=kLoop, calls=%fused_computation | loop fusion | flops 1048576 | bytes 1310720 | tf_op jit(solution)/shard_map/convert_element_type | solution.py:235
  47.3 2.7 %all-to-all-done.1 = bf16[4,2,512]{2,1,0:T(2,128)(2,1)S(1)} async-done(((bf16[4,2,512]{2,1,0:T(2,128)(2,1)}), bf16[4,2,512]{2,1,0:T(2,128)(2,1)S(1)}, u32[]{:S(2)}, u32[]{:S(2)}) %all-to-all-start.1) | async-done | bytes 8224 | tf_op jit(solution)/shard_map/all_to_all | solution.py:230
  50.0 0.6 %reduce_sum.12 = bf16[2,512]{1,0:T(2,128)(2,1)} reduce(bf16[4,2,512]{2,1,0:T(2,128)(2,1)S(1)} %all-to-all-done.1, bf16[]{:T(256)} %constant.8.clone.1), dimensions={0}, to_apply=%region_0.0 | reduce | flops 3072 | bytes 10242 | tf_op jit(solution)/shard_map/reduce_sum | solution.py:231
Async XLA Ops:
  3.2 33.7 %all-to-all-start = ((bf16[128,2,384]{2,1,0:T(2,128)(2,1)}), bf16[128,2,384]{2,1,0:T(2,128)(2,1)S(1)}, u32[]{:S(2)}, u32[]{:S(2)}) async-start(bf16[128,2,384]{2,1,0:T(2,128)(2,1)} %shard_map.141), calls=%async_computation | async-start | bytes 393216 | tf_op jit(solution)/shard_map/all_to_all | solution.py:192
  24.3 22.1 %copy-start.1 = (bf16[256,512]{1,0:T(8,128)(2,1)S(1)}, bf16[256,512]{1,0:T(8,128)(2,1)}, u32[]{:S(2)}) copy-start(bf16[256,512]{1,0:T(8,128)(2,1)} %get-tuple-element.11) | copy-start | bytes 786436
  24.3 20.3 %collective-permute-start.2 = (bf16[256,512]{1,0:T(8,128)(2,1)}, bf16[256,512]{1,0:T(8,128)(2,1)S(1)}, u32[]{:S(2)}, u32[]{:S(2)}) collective-permute-start(bf16[256,512]{1,0:T(8,128)(2,1)} %get-tuple-element.14), channel_id=1, source_target_pairs={{0,3},{1,0},{2,1},{3,2},{4,7},{5,4},{6,5},{7,6},{8,11},{9,8},{10,9... | collective-permute-start | bytes 786440 | tf_op jit(solution)/shard_map/ppermute | solution.py:204
  29.1 15.5 %collective-permute-start.1 = (bf16[256,512]{1,0:T(8,128)(2,1)}, bf16[256,512]{1,0:T(8,128)(2,1)S(1)}, u32[]{:S(2)}, u32[]{:S(2)}) collective-permute-start(bf16[256,512]{1,0:T(8,128)(2,1)} %get-tuple-element.13), channel_id=1, source_target_pairs={{0,2},{1,3},{2,0},{3,1},{4,6},{5,7},{6,4},{7,5},{8,10},{9,11},{10,... | collective-permute-start | bytes 786440 | tf_op jit(solution)/shard_map/ppermute | solution.py:204
  31.8 14.6 %collective-permute-start = (bf16[256,512]{1,0:T(8,128)(2,1)}, bf16[256,512]{1,0:T(8,128)(2,1)S(1)}, u32[]{:S(2)}, u32[]{:S(2)}) collective-permute-start(bf16[256,512]{1,0:T(8,128)(2,1)} %get-tuple-element.12), channel_id=1, source_target_pairs={{0,1},{1,2},{2,3},{3,0},{4,5},{5,6},{6,7},{7,4},{8,9},{9,10},{10,1... | collective-permute-start | bytes 786440 | tf_op jit(solution)/shard_map/ppermute | solution.py:204
  36.9 0.7 %copy-start = (bf16[128,2,384]{2,1,0:T(2,128)(2,1)}, bf16[128,2,384]{2,1,0:T(2,128)(2,1)S(1)}, u32[]{:S(2)}) copy-start(bf16[128,2,384]{2,1,0:T(2,128)(2,1)S(1)} %all-to-all-done.got) | copy-start | bytes 589828
  41.0 8.9 %all-to-all-start.1 = ((bf16[4,2,512]{2,1,0:T(2,128)(2,1)}), bf16[4,2,512]{2,1,0:T(2,128)(2,1)S(1)}, u32[]{:S(2)}, u32[]{:S(2)}) async-start(bf16[4,2,512]{2,1,0:T(2,128)(2,1)} %shard_map.143), calls=%async_computation.1 | async-start | bytes 16384 | tf_op jit(solution)/shard_map/all_to_all | solution.py:230

commit v3 on v2

--- a/solution.py
+++ b/solution.py
@@ -1,3 +1,5 @@
+import functools
+
 import jax
 import jax.numpy as jnp
 import numpy as np
@@ -8,6 +10,7 @@
 
 CAP = 2
 ROPE_BASE = 600000.0
+VMEM_LIMIT = 16 * 2**20
 F32 = jnp.float32
 BF16 = jnp.bfloat16
 
@@ -16,32 +19,96 @@
     return lax.dot_general(a, b, (((ca,), (cb,)), ((), ())), preferred_element_type=F32)
 
 
-def call(kernel, outs, *args, scalars=()):
+def near(x):
+    return pltpu.with_memory_space_constraint(x, pltpu.VMEM)
+
+
+def call(kernel, outs, *args):
     vmem = pl.BlockSpec(memory_space=pltpu.VMEM)
-    smem = pl.BlockSpec(memory_space=pltpu.SMEM)
     return pl.pallas_call(
         kernel,
         out_shape=outs,
-        in_specs=[smem] * len(scalars) + [vmem] * len(args),
+        in_specs=[vmem] * len(args),
         out_specs=jax.tree.map(lambda _: vmem, outs),
-    )(*scalars, *args)
-
-
-def pack_kernel(hidden, weight, dest, out):
-    peers, cap, width = out.shape
-    rows = hidden.shape[0]
-    rebuilt = dot(hidden[...], weight[...], 1, 0).astype(BF16)
+        compiler_params=pltpu.CompilerParams(vmem_limit_bytes=VMEM_LIMIT),
+    )(*args)
+
+
+def pack_kernel(count, *refs):
+    hidden, weight, dest = refs[:3]
+    later = refs[3 : 3 + count]
+    out = refs[3 + count]
+    kept = refs[4 + count : 4 + 2 * count]
+    hidden_v, weight_v, dest_v, out_v, sem, later_sem = refs[4 + 2 * count :]
+    peers, cap, _ = out.shape
+    rows, depth = hidden.shape
+    steps = 4
+    step = depth // steps
+    copies = [pltpu.make_async_copy(dest, dest_v, sem.at[2 * steps])]
+    for k in range(steps):
+        part = pl.ds(k * step, step)
+        copies.append(pltpu.make_async_copy(hidden.at[:, part], hidden_v.at[:, part], sem.at[2 * k]))
+        copies.append(pltpu.make_async_copy(weight.at[part], weight_v.at[part], sem.at[2 * k + 1]))
+    copies += [
+        pltpu.make_async_copy(x, y, later_sem.at[i])
+        for i, (x, y) in enumerate(zip(later, kept, strict=True))
+    ]
+    own = 1 + 2 * steps
+    for copy in copies[:own]:
+        copy.start()
+    copies[0].wait()
     number = lax.broadcasted_iota(jnp.int32, (1, rows), 1)
-    code = dest[...] * cap + number % cap
-    code = jnp.where(dest[...] >= 0, code, -1)
+    code = dest_v[...] * cap + number % cap
+    code = jnp.where(dest_v[...] >= 0, code, -1)
     place = lax.broadcasted_iota(jnp.int32, (peers * cap, rows), 0)
     chosen = jnp.where(place == code, 1.0, 0.0).astype(BF16)
-    packed = dot(chosen, rebuilt, 1, 0).astype(BF16)
+    rebuilt = jnp.zeros((rows, weight.shape[1]), F32)
+    for k in range(steps):
+        copies[1 + 2 * k].wait()
+        copies[2 + 2 * k].wait()
+        if k == steps - 1:
+            for copy in copies[own:]:
+                copy.start()
+        part = slice(k * step, (k + 1) * step)
+        rebuilt = rebuilt + dot(hidden_v[:, part], weight_v[part], 1, 0)
+    packed = dot(chosen, rebuilt.astype(BF16), 1, 0).astype(BF16)
     both = jnp.concatenate([packed, chosen], axis=1)
-    out[...] = both.reshape(peers, cap, width)
-
-
-def prompt_kernel(place, query, key_value, segment, weight, *outs):
+    out_v[...] = both.reshape(out.shape)
+    send = pltpu.make_async_copy(out_v, out, sem.at[2 * steps + 1])
+    send.start()
+    for copy in copies[own:]:
+        copy.wait()
+    send.wait()
+
+
+def pack(peers, hidden, weight, dest, *later):
+    shape = (peers, CAP, weight.shape[1] + hidden.shape[0])
+    vmem = pl.BlockSpec(memory_space=pltpu.VMEM)
+    hbm = pl.BlockSpec(memory_space=pl.ANY)
+    far = [
+        pltpu.with_memory_space_constraint(x, pltpu.HBM)
+        for x in (hidden, weight, dest, *later)
+    ]
+    send, *kept = pl.pallas_call(
+        functools.partial(pack_kernel, len(later)),
+        out_shape=[jax.ShapeDtypeStruct(shape, BF16)]
+        + [pltpu.VMEM(x.shape, x.dtype) for x in later],
+        in_specs=[hbm] * len(far),
+        out_specs=[hbm] + [vmem] * len(later),
+        scratch_shapes=[
+            pltpu.VMEM(hidden.shape, BF16),
+            pltpu.VMEM(weight.shape, BF16),
+            pltpu.VMEM(dest.shape, dest.dtype),
+            pltpu.VMEM(shape, BF16),
+            pltpu.SemaphoreType.DMA((10,)),
+            pltpu.SemaphoreType.DMA((len(later),)),
+        ],
+        compiler_params=pltpu.CompilerParams(vmem_limit_bytes=VMEM_LIMIT),
+    )(*far)
+    return send, kept
+
+
+def prompt_kernel(query, key_value, segment, weight, *outs):
     tokens, _ = query.shape
     head = key_value.shape[1] // 2
     groups = query.shape[1] // head
@@ -66,7 +133,7 @@
         mixed.append((mix / total).astype(BF16))
     mixed = jnp.concatenate(mixed, axis=1)
     for k in range(parts):
-        to = lax.rem(place[0] + k, parts)
+        to = lax.rem(lax.axis_index("tp") + k, parts)
         columns = pl.ds(pl.multiple_of(to * share, share), share)
         outs[k][...] = dot(mixed, weight[:, columns], 1, 0).astype(BF16)
 
@@ -94,9 +161,9 @@
     col = lax.broadcasted_iota(jnp.int32, (rows, cache.shape[0]), 1)
     decoder = row % decoders
     offset = col - decoder * cache_len
-    limit = jnp.full_like(row, length[0])
+    limit = length[:, :1]
     for b in range(1, decoders):
-        limit = jnp.where(decoder == b, length[b], limit)
+        limit = jnp.where(decoder == b, length[:, b : b + 1], limit)
     live = (offset >= 0) & (offset < limit) & (offset < cache_len) & (hit < 0.5)
     scores = dot(q, cache[:, :head], 1, 1) * scale
     scores = jnp.where(live, scores, -jnp.inf)
@@ -121,13 +188,12 @@
     sin_o[...] = jnp.where(lane < head // 2, -sine, sine)
 
 
-def after_kernel(length, got, query, slots, top_i, total_i, mix_i, cos_i, sin_i, weight, out):
+def after_kernel(cache_len, length, got, query, slots, top_i, total_i, mix_i, cos_i, sin_i, weight, out):
     peers, cap, width = got.shape
     listed = slots.shape[1]
     head = mix_i.shape[1]
     decoders = query.shape[0]
     parts, _, share = out.shape
-    cache_len = 512
     scale = head**-0.5
     flat = got[...].reshape(peers * cap, width)
     ordered = dot(flat[:, 2 * head :], flat[:, : 2 * head], 0, 0)
@@ -139,9 +205,9 @@
     scores = dot(q, turned, 1, 1) * scale
     row = lax.broadcasted_iota(jnp.int32, (rows, listed), 0)
     decoder = row % decoders
-    limit = jnp.full_like(row, length[0])
+    limit = length[:, :1]
     for b in range(1, decoders):
-        limit = jnp.where(decoder == b, length[b], limit)
+        limit = jnp.where(decoder == b, length[:, b : b + 1], limit)
     offset = slots[...] - decoder * cache_len
     live = (slots[...] >= 0) & (offset >= 0) & (offset < limit) & (offset < cache_len)
     scores = jnp.where(live, scores, -jnp.inf)
@@ -156,6 +222,14 @@
     ).astype(BF16)
     for t in range(parts):
         out[t] = dot(mixed, weight[:, t * share : (t + 1) * share], 1, 0).astype(BF16)
+
+
+def sum_kernel(*refs):
+    *parts, out = refs
+    total = parts[0][...].astype(F32)
+    for part in parts[1:]:
+        total = total + part[...].astype(F32)
+    out[...] = total.astype(BF16)
 
 
 def shards(
@@ -182,57 +256,65 @@
     share = out_weight.shape[1] // parts
     shape = jax.ShapeDtypeStruct
 
-    send = call(
-        pack_kernel,
-        shape((peers, CAP, pair + listed), BF16),
+    half = head // 2
+    frequency = (ROPE_BASE ** (-2.0 * (np.arange(head) % half) / head)).astype(np.float32)
+    send, kept = pack(
+        peers,
         rebuild_hidden_state,
         key_value_weight.reshape(-1, pair),
         owner_dest,
-    )
-    got = lax.all_to_all(send, "req", split_axis=0, concat_axis=0, tiled=True)
-
-    prompt_part = call(
-        prompt_kernel,
-        [shape((tokens, share), BF16)] * parts,
         prompt_query,
         prompt_key_value.reshape(tokens, pair),
         prompt_segment_index,
         out_weight,
-        scalars=(lax.axis_index("tp").reshape(1),),
+        key_value_cache.reshape(-1, pair),
+        live_cache_length.reshape(1, decoders),
+        decoder_query,
+        decoder_key_value.reshape(decoders, pair),
+        miss_pos,
+        jnp.asarray(frequency).reshape(1, head),
+    )
+    got = lax.all_to_all(send, "req", split_axis=0, concat_axis=0, tiled=True)
+    query_v, key_value_v, segment_v, weight_v, cache_v, length_v, dec_query_v, own_v, slots_v, frequency_v = map(near, kept)
+
+    prompt_part = call(
+        prompt_kernel,
+        [shape((tokens, share), BF16)] * parts,
+        query_v,
+        key_value_v,
+        segment_v,
+        weight_v,
     )
     arrived = [
         lax.ppermute(prompt_part[k], "tp", [(i, (i + k) % parts) for i in range(parts)])
         for k in range(1, parts)
     ]
-    half = head // 2
-    frequency = (ROPE_BASE ** (-2.0 * (np.arange(head) % half) / head)).astype(np.float32)
     rows = decoder_query.shape[1] // head * decoders
     state = call(
         before_kernel,
-        [shape((rows, head), F32)] * 3 + [shape((listed, head), F32)] * 2,
-        decoder_query,
-        decoder_key_value.reshape(decoders, pair),
-        key_value_cache.reshape(-1, pair),
-        miss_pos,
-        jnp.asarray(frequency).reshape(1, head),
-        scalars=(live_cache_length,),
+        [pltpu.VMEM((rows, head), F32)] * 3 + [pltpu.VMEM((listed, head), F32)] * 2,
+        length_v,
+        dec_query_v,
+        own_v,
+        cache_v,
+        slots_v,
+        frequency_v,
     )
     dec_part = call(
-        after_kernel,
+        functools.partial(after_kernel, key_value_cache.shape[1]),
         shape((parts, decoders, share), BF16),
-        got,
-        decoder_query,
-        miss_pos,
-        *state,
-        out_weight,
-        scalars=(live_cache_length,),
+        length_v,
+        near(got),
+        dec_query_v,
+        slots_v,
+        *map(near, state),
+        weight_v,
     )
     dec_got = lax.all_to_all(dec_part, "tp", split_axis=0, concat_axis=0, tiled=True)
     dec_out = jnp.sum(dec_got.astype(F32), axis=0).astype(BF16)
-    prompt_out = prompt_part[0].astype(F32)
-    for part in arrived:
-        prompt_out = prompt_out + part.astype(F32)
-    prompt_out = prompt_out.astype(BF16)
+    prompt_out = call(
+        sum_kernel, shape((tokens, share), BF16), prompt_part[0], *map(near, arrived)
+    )
     return prompt_out, dec_out
 
 

time: 51 us -> 47.5 us (0.931)
  the two profiles are of different devices: /device:TPU:8 before, /device:TPU:11 now
where the time goes in v3:
time: 47.5 us; the launch traced here: 47.1 us
  starting transfers between devices  31.6 us (67%)
  Pallas kernels  9.63 us (20%)
  waiting for transfers between devices  4.6 us (10%)
  between operations  0.68 us (1%)
  other arithmetic  0.6 us (1%)
    all_to_all x1, starting transfers between devices, shards(): got = lax.all_to_all(send, 'req', split_axis=0, concat_axis=0, tiled=True)  17.7 us
    ppermute x3, starting transfers between devices, shards(): lax.ppermute(prompt_part[k], 'tp', [(i, (i + k) % parts) for i in range(p...  9.63 us
    pallas_call x4, Pallas kernels, call(): pl.pallas_call(kernel, out_shape=outs, in_specs=[vmem] * len(args), out_s...  5.99 us
    all_to_all x1, starting transfers between devices, shards(): lax.all_to_all(dec_part, 'tp', split_axis=0, concat_axis=0, tiled=True)  4.26 us
    ppermute x3, waiting for transfers between devices, shards(): lax.ppermute(prompt_part[k], 'tp', [(i, (i + k) % parts) for i in range(p...  3.68 us
    pallas_call x1, Pallas kernels, pack(): pl.pallas_call(functools.partial(pack_kernel, len(later)), out_shape=[jax...  3.64 us
  transfers between devices with their start and end apart: 5, of which 2 were waited for; matrix products, arithmetic and copies ran while one was open for 0% of the time, Pallas kernels for 13%

profile of v3, /device:TPU:11, one launch (start us, length us, event | category | flops | bytes accessed | tf_op | source)
XLA Modules:
  0.0 47.1 jit_solution(3259243008027704155)
XLA Ops:
  0.6 3.6 %shard_map.140 = (bf16[128,2,384]{2,1,0:T(2,128)(2,1)}, bf16[256,512]{1,0:T(8,128)(2,1)S(1)}, bf16[256,256]{1,0:T(8,128)(2,1)S(1)}, s32[1,256]{1,0:T(1,128)S(1)}...) custom-call(bf16[128,2048]{1,0:T(8,128)(2,1)} %refs_0_.1, ...), custom_call_target="tpu_custom_call" | custom-call | tf_op jit(solution)/shard_map/pallas_call | solution.py:92
  4.3 17.7 %all-to-all-start = ((bf16[128,2,384]{2,1,0:T(2,128)(2,1)}), bf16[128,2,384]{2,1,0:T(2,128)(2,1)S(1)}, u32[]{:S(2)}, u32[]{:S(2)}) async-start(bf16[128,2,384]{2,1,0:T(2,128)(2,1)} %get-tuple-element.31), calls=%async_computation | async-start | bytes 393216 | tf_op jit(solution)/shard_map/all_to_all | solution.py:277
  22.0 2.0 %shard_map.141 = (bf16[256,512]{1,0:T(8,128)(2,1)S(1)}, bf16[256,512]{1,0:T(8,128)(2,1)}, bf16[256,512]{1,0:T(8,128)(2,1)}, bf16[256,512]{1,0:T(8,128)(2,1)}) custom-call(bf16[256,512]{1,0:T(8,128)(2,1)S(1)} %get-tuple-element.22.query, bf16[256,256]{1,0:T(8,128)(2,1)S(1)} %get-tuple-element.23.key_value, s32[1,256]{1,0:T(1,128)S(1)} %get-tuple-element.24.segment, ...), custom_call_target="tpu_custom_call" | custom-call | tf_op jit(solution)/shard_map/pallas_call | solution.py:28
  23.9 3.1 %collective-permute-start = (bf16[256,512]{1,0:T(8,128)(2,1)}, bf16[256,512]{1,0:T(8,128)(2,1)S(1)}, u32[]{:S(2)}, u32[]{:S(2)}) collective-permute-start(bf16[256,512]{1,0:T(8,128)(2,1)} %get-tuple-element.27), channel_id=1, source_target_pairs={{0,1},{1,2},{2,3},{3,0},{4,5},{5,6},{6,7},{7,4},{8,9},{9,10},{10,1... | collective-permute-start | bytes 786440 | tf_op jit(solution)/shard_map/ppermute | solution.py:289
  27.0 2.7 %collective-permute-start.1 = (bf16[256,512]{1,0:T(8,128)(2,1)}, bf16[256,512]{1,0:T(8,128)(2,1)}, u32[]{:S(2)}, u32[]{:S(2)}) collective-permute-start(bf16[256,512]{1,0:T(8,128)(2,1)} %get-tuple-element.28), channel_id=1, source_target_pairs={{0,2},{1,3},{2,0},{3,1},{4,6},{5,7},{6,4},{7,5},{8,10},{9,11},{10,... | collective-permute-start | bytes 786440 | tf_op jit(solution)/shard_map/ppermute | solution.py:289
  29.8 3.8 %collective-permute-start.2 = (bf16[256,512]{1,0:T(8,128)(2,1)}, bf16[256,512]{1,0:T(8,128)(2,1)}, u32[]{:S(2)}, u32[]{:S(2)}) collective-permute-start(bf16[256,512]{1,0:T(8,128)(2,1)} %get-tuple-element.29), channel_id=1, source_target_pairs={{0,3},{1,0},{2,1},{3,2},{4,7},{5,4},{6,5},{7,6},{8,11},{9,8},{10,9... | collective-permute-start | bytes 786440 | tf_op jit(solution)/shard_map/ppermute | solution.py:289
  33.6 0.6 %shard_map.143 = (f32[8,128]{1,0:T(8,128)S(1)}, f32[8,128]{1,0:T(8,128)S(1)}, f32[8,128]{1,0:T(8,128)S(1)}, f32[128,128]{1,0:T(8,128)S(1)}, f32[128,128]{1,0:T(8,128)S(1)}) custom-call(s32[1,2]{1,0:T(1,128)S(1)} %get-tuple-element.30.length, bf16[2,512]{1,0:T(2,128)(2,1)S(1)} %get-tuple-element.32.query, bf16[2,256]{1,0:T(2,128)(2,1)S(1)} %get-tuple-element.34.own, ...), custom_call_target="tpu_custom_call" | custom-call | tf_op jit(solution)/shard_map/pallas_call | solution.py:28
  34.2 0.9 %all-to-all-done.got = bf16[128,2,384]{2,1,0:T(2,128)(2,1)S(1)} async-done(((bf16[128,2,384]{2,1,0:T(2,128)(2,1)}), bf16[128,2,384]{2,1,0:T(2,128)(2,1)S(1)}, u32[]{:S(2)}, u32[]{:S(2)}) %all-to-all-start) | async-done | bytes 196640 | tf_op jit(solution)/shard_map/all_to_all | solution.py:277
  35.1 1.6 %shard_map.144 = bf16[4,2,512]{2,1,0:T(2,128)(2,1)} custom-call(s32[1,2]{1,0:T(1,128)S(1)} %get-tuple-element.30.length, bf16[128,2,384]{2,1,0:T(2,128)(2,1)S(1)} %all-to-all-done.got, bf16[2,512]{1,0:T(2,128)(2,1)S(1)} %get-tuple-element.32.query, s32[1,128]{1,0:T(1,128)S(1)} %get-tuple-element.33.slots, f32[8,128]{1,0:T(8,128)S(1)} %get-tuple-element.37.top_i, ...), custom_call_target="tpu_custom_call" | custom-call | tf_op jit(solution)/shard_map/pallas_call | solution.py:28
  36.7 4.3 %all-to-all-start.1 = ((bf16[4,2,512]{2,1,0:T(2,128)(2,1)}), bf16[4,2,512]{2,1,0:T(2,128)(2,1)S(1)}, u32[]{:S(2)}, u32[]{:S(2)}) async-start(bf16[4,2,512]{2,1,0:T(2,128)(2,1)} %shard_map.144), calls=%async_computation.1 | async-start | bytes 16384 | tf_op jit(solution)/shard_map/all_to_all | solution.py:313
  41.0 0.0 collective-permute-done.refs_1_
  41.0 0.0 collective-permute-done.1.refs_2_
  41.0 3.7 %collective-permute-done.2.refs_3_ = bf16[256,512]{1,0:T(8,128)(2,1)} collective-permute-done((bf16[256,512]{1,0:T(8,128)(2,1)}, bf16[256,512]{1,0:T(8,128)(2,1)}, u32[]{:S(2)}, u32[]{:S(2)}) %collective-permute-start.2) | collective-permute-done | bytes 262176 | tf_op jit(solution)/shard_map/ppermute | solution.py:289
  44.6 1.9 %shard_map.142 = bf16[256,512]{1,0:T(8,128)(2,1)} custom-call(bf16[256,512]{1,0:T(8,128)(2,1)S(1)} %get-tuple-element.26.refs_0_, bf16[256,512]{1,0:T(8,128)(2,1)S(1)} %collective-permute-done.refs_1_, bf16[256,512]{1,0:T(8,128)(2,1)} %collective-permute-done.1.refs_2_, bf16[256,512]{1,0:T(8,128)(2,1)} %collective-permute-done.2.refs_3_), custom_call_target="tpu_custom_call" | custom-call | tf_op jit(solution)/shard_map/pallas_call | solution.py:28
  46.5 0.0 all-to-all-done.1
  46.5 0.6 %reduce_sum.12 = bf16[2,512]{1,0:T(2,128)(2,1)} reduce(bf16[4,2,512]{2,1,0:T(2,128)(2,1)S(1)} %all-to-all-done.1, bf16[]{:T(256)} %constant.4.clone.1), dimensions={0}, to_apply=%region_0.0 | reduce | flops 3072 | bytes 10242 | tf_op jit(solution)/shard_map/reduce_sum | solution.py:314
Async XLA Ops:
  4.3 30.8 %all-to-all-start = ((bf16[128,2,384]{2,1,0:T(2,128)(2,1)}), bf16[128,2,384]{2,1,0:T(2,128)(2,1)S(1)}, u32[]{:S(2)}, u32[]{:S(2)}) async-start(bf16[128,2,384]{2,1,0:T(2,128)(2,1)} %get-tuple-element.31), calls=%async_computation | async-start | bytes 393216 | tf_op jit(solution)/shard_map/all_to_all | solution.py:277
  23.9 17.0 %collective-permute-start = (bf16[256,512]{1,0:T(8,128)(2,1)}, bf16[256,512]{1,0:T(8,128)(2,1)S(1)}, u32[]{:S(2)}, u32[]{:S(2)}) collective-permute-start(bf16[256,512]{1,0:T(8,128)(2,1)} %get-tuple-element.27), channel_id=1, source_target_pairs={{0,1},{1,2},{2,3},{3,0},{4,5},{5,6},{6,7},{7,4},{8,9},{9,10},{10,1... | collective-permute-start | bytes 786440 | tf_op jit(solution)/shard_map/ppermute | solution.py:289
  27.0 13.9 %collective-permute-start.1 = (bf16[256,512]{1,0:T(8,128)(2,1)}, bf16[256,512]{1,0:T(8,128)(2,1)}, u32[]{:S(2)}, u32[]{:S(2)}) collective-permute-start(bf16[256,512]{1,0:T(8,128)(2,1)} %get-tuple-element.28), channel_id=1, source_target_pairs={{0,2},{1,3},{2,0},{3,1},{4,6},{5,7},{6,4},{7,5},{8,10},{9,11},{10,... | collective-permute-start | bytes 786440 | tf_op jit(solution)/shard_map/ppermute | solution.py:289
  29.8 14.8 %collective-permute-start.2 = (bf16[256,512]{1,0:T(8,128)(2,1)}, bf16[256,512]{1,0:T(8,128)(2,1)}, u32[]{:S(2)}, u32[]{:S(2)}) collective-permute-start(bf16[256,512]{1,0:T(8,128)(2,1)} %get-tuple-element.29), channel_id=1, source_target_pairs={{0,3},{1,0},{2,1},{3,2},{4,7},{5,4},{6,5},{7,6},{8,11},{9,8},{10,9... | collective-permute-start | bytes 786440 | tf_op jit(solution)/shard_map/ppermute | solution.py:289
  36.7 9.8 %all-to-all-start.1 = ((bf16[4,2,512]{2,1,0:T(2,128)(2,1)}), bf16[4,2,512]{2,1,0:T(2,128)(2,1)S(1)}, u32[]{:S(2)}, u32[]{:S(2)}) async-start(bf16[4,2,512]{2,1,0:T(2,128)(2,1)} %shard_map.144), calls=%async_computation.1 | async-start | bytes 16384 | tf_op jit(solution)/shard_map/all_to_all | solution.py:313

commit v4 on v1

v4 whole, which is shorter than its diff:
```python
import functools

import jax
import jax.numpy as jnp
import numpy as np
from jax import lax
from jax.experimental import pallas as pl
from jax.experimental.pallas import tpu as pltpu
from jax.sharding import PartitionSpec as P

CAP = 2
ROPE_BASE = 600000.0
VMEM_LIMIT = 16 * 2**20
F32 = jnp.float32
BF16 = jnp.bfloat16


def dot(a, b, ca, cb):
    return lax.dot_general(a, b, (((ca,), (cb,)), ((), ())), preferred_element_type=F32)


def like(x):
    return pltpu.VMEM(x.shape, x.dtype)


def near(x):
    return pltpu.with_memory_space_constraint(x, pltpu.VMEM)


def call(kernel, outs, *args, far=(), scratch=(), far_out=0):
    vmem = pl.BlockSpec(memory_space=pltpu.VMEM)
    hbm = pl.BlockSpec(memory_space=pl.ANY)
    return pl.pallas_call(
        kernel,
        out_shape=list(outs),
        in_specs=[vmem] * len(args) + [hbm] * len(far),
        out_specs=[hbm] * far_out + [vmem] * (len(outs) - far_out),
        scratch_shapes=scratch,
        compiler_params=pltpu.CompilerParams(vmem_limit_bytes=VMEM_LIMIT),
    )(*map(near, args), *[pltpu.with_memory_space_constraint(x, pltpu.HBM) for x in far])


def start_all(far, near_refs, sem):
    copies = [
        pltpu.make_async_copy(x, y, sem.at[i]) for i, (x, y) in enumerate(zip(far, near_refs, strict=True))
    ]
    for copy in copies:
        copy.start()
    return copies


def columns_for(k, share, parts):
    to = lax.bitwise_xor(lax.axis_index("tp"), k)
    return pl.ds(pl.multiple_of(to * share, share), share)


def pack_kernel(hidden, weight, dest, out, hidden_v, weight_v, dest_v, out_v, sem):
    peers, cap, width = out.shape
    rows, depth = hidden.shape
    steps, halves = 4, 2
    part = [pl.ds(k * depth // steps, depth // steps) for k in range(steps)]
    copies = start_all(
        [dest, *[x for p in part for x in (hidden.at[:, p], weight.at[p])]],
        [dest_v, *[x for p in part for x in (hidden_v.at[:, p], weight_v.at[p])]],
        sem,
    )
    copies[0].wait()
    number = lax.broadcasted_iota(jnp.int32, (1, rows), 1)
    code = dest_v[...] * cap + number % cap
    code = jnp.where(dest_v[...] >= 0, code, -1)
    place = lax.broadcasted_iota(jnp.int32, (peers * cap, rows), 0)
    chosen = jnp.where(place == code, 1.0, 0.0).astype(BF16)
    rebuilt = jnp.zeros((rows, weight.shape[1]), F32)
    for k, p in enumerate(part):
        copies[1 + 2 * k].wait()
        copies[2 + 2 * k].wait()
        rebuilt = rebuilt + dot(hidden_v[:, p], weight_v[p], 1, 0)
    rebuilt = rebuilt.astype(BF16)
    sends = []
    for h in range(halves):
        size = peers // halves
        mine = chosen[h * size * cap : (h + 1) * size * cap]
        packed = dot(mine, rebuilt, 1, 0).astype(BF16)
        own = pl.ds(h * size, size)
        out_v[own] = jnp.concatenate([packed, mine], axis=1).reshape(size, cap, width)
        sends.append(pltpu.make_async_copy(out_v.at[own], out.at[own], sem.at[1 + 2 * steps + h]))
        sends[-1].start()
    for send in sends:
        send.wait()


def middle_kernel(parts, query, key_value, segment, weight, *refs):
    blocks = 8
    far, outs, weight_o = refs[:6], refs[6 : 13 + parts], refs[13 + parts]
    held, sem = refs[14 + parts : 23 + parts], refs[23 + parts]
    step = weight.shape[0] // blocks
    block = [pl.ds(i * step, step) for i in range(blocks)]
    copies = start_all(
        [query, key_value, segment, *[weight.at[x] for x in block], *far],
        [*held[:3], *[weight_o.at[x] for x in block], *held[3:]],
        sem,
    )
    for copy in copies[:3]:
        copy.wait()
    mixed = prompt_rows(*held[:3])
    for copy in copies[3:]:
        copy.wait()
    share = outs[0].shape[1]
    for k in range(parts):
        outs[k][...] = dot(mixed, weight_o[:, columns_for(k, share, parts)], 1, 0).astype(BF16)
    cache_rows(*held[3:], *outs[parts:])


def prompt_rows(query, key_value, segment):
    tokens, _ = query.shape
    head = key_value.shape[1] // 2
    groups = query.shape[1] // head
    scale = head**-0.5
    same = jnp.where(
        lax.broadcasted_iota(jnp.int32, (8, tokens), 0) == segment[...], 1.0, 0.0
    ).astype(BF16)
    same = dot(same, same, 0, 0)
    row = lax.broadcasted_iota(jnp.int32, (tokens, tokens), 0)
    col = lax.broadcasted_iota(jnp.int32, (tokens, tokens), 1)
    allowed = (same > 0.5) & (col <= row)
    keys = key_value[:, :head]
    values = key_value[:, head:]
    mixed = []
    for g in range(groups):
        scores = dot(query[:, g * head : (g + 1) * head], keys, 1, 1) * scale
        scores = jnp.where(allowed, scores, -jnp.inf)
        power = jnp.exp(scores - jnp.max(scores, axis=1, keepdims=True))
        total = jnp.sum(power, axis=1, keepdims=True)
        mix = dot(power.astype(BF16), values, 1, 0)
        mixed.append((mix / total).astype(BF16))
    return jnp.concatenate(mixed, axis=1)


def queries_by_row(query, head):
    wide = query[...].astype(F32)
    groups = wide.shape[1] // head
    return jnp.concatenate(
        [wide[:, g * head : (g + 1) * head] for g in range(groups)], axis=0
    ).astype(BF16)


def cache_rows(cache, length, query, own, slots, frequency, query_o, live_o, top_o, total_o, mix_o, cos_o, sin_o):
    head = cache.shape[1] // 2
    decoders = query.shape[0]
    cache_len = cache.shape[0] // decoders
    scale = head**-0.5
    q = queries_by_row(query, head)
    rows = q.shape[0]
    listed = slots.shape[1]
    slot_col = jnp.broadcast_to(slots[...].astype(F32), (listed, listed)).T
    place = lax.broadcasted_iota(jnp.int32, (1, cache.shape[0]), 1).astype(F32)
    hit = jnp.max(jnp.where(slot_col[:, :1] == place, 1.0, 0.0), axis=0, keepdims=True)

    def is_live(slot):
        decoder = lax.broadcasted_iota(jnp.int32, (rows, slot.shape[1]), 0) % decoders
        offset = slot - decoder * cache_len
        limit = length[:, :1]
        for b in range(1, decoders):
            limit = jnp.where(decoder == b, length[:, b : b + 1], limit)
        return (offset >= 0) & (offset < limit) & (offset < cache_len)

    query_o[...] = q
    listed_live = is_live(slots[...]) & (slots[...] >= 0)
    live_o[...] = jnp.where(listed_live, 0.0, -jnp.inf)
    col = lax.broadcasted_iota(jnp.int32, (1, cache.shape[0]), 1)
    live = is_live(col) & (hit < 0.5)
    scores = dot(q, cache[:, :head], 1, 1) * scale
    scores = jnp.where(live, scores, -jnp.inf)
    pair = own[...].astype(F32)
    pair = jnp.concatenate([pair] * (rows // decoders), axis=0)
    self_score = jnp.sum(q.astype(F32) * pair[:, :head], axis=1, keepdims=True) * scale
    top = jnp.maximum(jnp.max(scores, axis=1, keepdims=True), self_score)
    power = jnp.exp(scores - top)
    own_power = jnp.exp(self_score - top)
    total = own_power + jnp.sum(power, axis=1, keepdims=True)
    mix = dot(power.astype(BF16), cache[:, head:], 1, 0)
    mix = mix + own_power.astype(BF16).astype(F32) * pair[:, head:]
    top_o[...] = jnp.broadcast_to(top, top_o.shape)
    total_o[...] = jnp.broadcast_to(total, total_o.shape)
    mix_o[...] = mix
    position = jnp.maximum(slot_col, 0.0)
    position = position - cache_len * jnp.floor(position * (1.0 / cache_len))
    angle = position * frequency[...]
    lane = lax.broadcasted_iota(jnp.int32, angle.shape, 1)
    cos_o[...] = jnp.cos(angle)
    sine = jnp.sin(angle)
    sin_o[...] = jnp.where(lane < head // 2, -sine, sine)


def after_kernel(decoders, got, query, live, top_i, total_i, mix_i, cos_i, sin_i, weight, out):
    peers, cap, width = got.shape
    rows, head = mix_i.shape
    parts, _, share = out.shape
    scale = head**-0.5
    flat = got[...].reshape(peers * cap, width)
    ordered = dot(flat[:, 2 * head :], flat[:, : 2 * head], 0, 0)
    key = ordered[:, :head]
    value = ordered[:, head:].astype(BF16)
    turned = (key * cos_i[...] + pltpu.roll(key, head // 2, 1) * sin_i[...]).astype(BF16)
    scores = dot(query[...], turned, 1, 1) * scale + live[...]
    top = jnp.maximum(top_i[...], jnp.max(scores, axis=1, keepdims=True))
    power = jnp.exp(scores - top)
    keep = jnp.exp(top_i[...] - top)
    total = keep * total_i[...] + jnp.sum(power, axis=1, keepdims=True)
    mix = keep * mix_i[...] + dot(power.astype(BF16), value, 1, 0)
    mix = mix / total
    mixed = jnp.concatenate(
        [mix[i : i + decoders] for i in range(0, rows, decoders)], axis=1
    ).astype(BF16)
    for t in range(parts):
        out[t] = dot(mixed, weight[:, t * share : (t + 1) * share], 1, 0).astype(BF16)


def sum_kernel(*refs):
    *parts, out = refs
    total = parts[0][...].astype(F32)
    for part in parts[1:]:
        total = total + part[...].astype(F32)
    out[...] = total.astype(BF16)


def shards(
    prompt_query,
    prompt_key_value,
    prompt_segment_index,
    decoder_query,
    decoder_key_value,
    key_value_cache,
    live_cache_length,
    rebuild_hidden_state,
    owner_dest,
    miss_pos,
    key_value_weight,
    out_weight,
):
    pair = prompt_key_value.shape[-1]
    head = pair // 2
    peers = lax.axis_size("req")
    parts = lax.axis_size("tp")
    decoders = key_value_cache.shape[0]
    tokens = prompt_query.shape[0]
    listed = rebuild_hidden_state.shape[0]
    share = out_weight.shape[1] // parts
    shape = jax.ShapeDtypeStruct

    half = head // 2
    frequency = (ROPE_BASE ** (-2.0 * (np.arange(head) % half) / head)).astype(np.float32)
    rows = decoder_query.shape[1] // head * decoders
    payload = (peers, CAP, pair + listed)
    far = (rebuild_hidden_state, key_value_weight.reshape(-1, pair), owner_dest)
    (send,) = call(
        pack_kernel,
        [shape(payload, BF16)],
        far=far,
        scratch=[*map(like, far), pltpu.VMEM(payload, BF16), pltpu.SemaphoreType.DMA((11,))],
        far_out=1,
    )
    got = lax.all_to_all(send, "req", split_axis=0, concat_axis=0, tiled=True)
    far = (
        prompt_query,
        prompt_key_value.reshape(tokens, pair),
        prompt_segment_index,
        out_weight,
        key_value_cache.reshape(-1, pair),
        live_cache_length.reshape(1, decoders),
        decoder_query,
        decoder_key_value.reshape(decoders, pair),
        miss_pos,
        jnp.asarray(frequency).reshape(1, head),
    )
    middle = call(
        functools.partial(middle_kernel, parts),
        [pltpu.VMEM((tokens, share), BF16)] * parts
        + [pltpu.VMEM((rows, head), BF16), pltpu.VMEM((rows, listed), F32)]
        + [pltpu.VMEM((rows, head), F32)] * 3
        + [pltpu.VMEM((listed, head), F32)] * 2
        + [like(out_weight)],
        far=far,
        scratch=[like(x) for x in far if x is not out_weight] + [pltpu.SemaphoreType.DMA((17,))],
    )
    prompt_part, state = middle[:parts], middle[parts:]
    arrived = [
        lax.ppermute(prompt_part[k], "tp", [(i, i ^ k) for i in range(parts)])
        for k in (2, 1, 3)
    ]
    (dec_part,) = call(
        functools.partial(after_kernel, decoders),
        [pltpu.VMEM((parts, decoders, share), BF16)],
        got,
        *state,
    )
    dec_got = lax.all_to_all(dec_part, "tp", split_axis=0, concat_axis=0, tiled=True)
    dec_out = jnp.sum(dec_got.astype(F32), axis=0).astype(BF16)
    (prompt_out,) = call(sum_kernel, [shape((tokens, share), BF16)], prompt_part[0], *arrived)
    return prompt_out, dec_out


def solution(mesh):
    in_specs = (
        P("req", "tp"),
        P("req", "tp", None),
        P("req", None),
        P("req", "tp"),
        P("req", "tp", None),
        P("req", None, "tp", None),
        P("req"),
        P("req", None),
        P("req", None),
        P("req", None),
        P(None, "tp", None),
        P("tp", None),
    )
    out_specs = (P("req", "tp"), P("req", "tp"))
    return jax.shard_map(shards, mesh=mesh, in_specs=in_specs, out_specs=out_specs, check_vma=False)
```

time: 67.1 us -> 46.3 us (0.69)
  the two profiles are of different devices: /device:TPU:8 before, /device:TPU:1 now
where the time goes in v4:
time: 46.3 us; the launch traced here: 46 us
  starting transfers between devices  31.8 us (69%)
  Pallas kernels  8.61 us (19%)
  waiting for transfers between devices  4.31 us (9%)
  between operations  0.68 us (1%)
  other arithmetic  0.59 us (1%)
    all_to_all x1, starting transfers between devices, shards(): got = lax.all_to_all(send, 'req', split_axis=0, concat_axis=0, tiled=True)  18.4 us
    ppermute x3, starting transfers between devices, shards(): lax.ppermute(prompt_part[k], 'tp', [(i, i ^ k) for i in range(parts)])  9.33 us
    pallas_call x4, Pallas kernels, call(): pl.pallas_call(kernel, out_shape=list(outs), in_specs=[vmem] * len(args)...  8.61 us
    all_to_all x1, starting transfers between devices, shards(): lax.all_to_all(dec_part, 'tp', split_axis=0, concat_axis=0, tiled=True)  4.01 us
    all_to_all x1, waiting for transfers between devices, shards(): lax.all_to_all(dec_part, 'tp', split_axis=0, concat_axis=0, tiled=True)  2.27 us
    ppermute x3, waiting for transfers between devices, shards(): lax.ppermute(prompt_part[k], 'tp', [(i, i ^ k) for i in range(parts)])  1.07 us
    all_to_all x1, waiting for transfers between devices, shards(): got = lax.all_to_all(send, 'req', split_axis=0, concat_axis=0, tiled=True)  0.97 us
  transfers between devices with their start and end apart: 5, of which 4 were waited for; matrix products, arithmetic and copies ran while one was open for 0% of the time, Pallas kernels for 13%

profile of v4, /device:TPU:1, one launch (start us, length us, event | category | flops | bytes accessed | tf_op | source)
XLA Modules:
  0.0 46.0 jit_solution(8716025690752728713)
XLA Ops:
  0.6 2.7 %shard_map.142 = bf16[128,2,384]{2,1,0:T(2,128)(2,1)} custom-call(bf16[128,2048]{1,0:T(8,128)(2,1)} %hidden.1, bf16[2048,256]{1,0:T(8,128)(2,1)} %bitcast.5, s32[1,128]{1,0:T(1,128)} %dest.1), custom_call_target="tpu_custom_call" | custom-call | tf_op jit(solution)/shard_map/pallas_call | solution.py:33
  3.3 18.4 %all-to-all-start = ((bf16[128,2,384]{2,1,0:T(2,128)(2,1)}), bf16[128,2,384]{2,1,0:T(2,128)(2,1)S(1)}, u32[]{:S(2)}, u32[]{:S(2)}) async-start(bf16[128,2,384]{2,1,0:T(2,128)(2,1)} %shard_map.142), calls=%async_computation | async-start | bytes 393216 | tf_op jit(solution)/shard_map/all_to_all | solution.py:263
  21.7 3.6 %shard_map.140 = (bf16[256,512]{1,0:T(8,128)(2,1)S(1)}, bf16[256,512]{1,0:T(8,128)(2,1)}, bf16[256,512]{1,0:T(8,128)(2,1)}, bf16[256,512]{1,0:T(8,128)(2,1)}, bf...) custom-call(bf16[256,512]{1,0:T(8,128)(2,1)} %query.1, ...), custom_call_target="tpu_custom_call" | custom-call | tf_op jit(solution)/shard_map/pallas_call | solution.py:33
  25.3 4.6 %collective-permute-start = (bf16[256,512]{1,0:T(8,128)(2,1)}, bf16[256,512]{1,0:T(8,128)(2,1)S(1)}, u32[]{:S(2)}, u32[]{:S(2)}) collective-permute-start(bf16[256,512]{1,0:T(8,128)(2,1)} %get-tuple-element.15), channel_id=1, source_target_pairs={{0,2},{1,3},{2,0},{3,1},{4,6},{5,7},{6,4},{7,5},{8,10},{9,11},{10,... | collective-permute-start | bytes 786440 | tf_op jit(solution)/shard_map/ppermute | solution.py:288
  30.0 2.2 %collective-permute-start.1 = (bf16[256,512]{1,0:T(8,128)(2,1)}, bf16[256,512]{1,0:T(8,128)(2,1)S(1)}, u32[]{:S(2)}, u32[]{:S(2)}) collective-permute-start(bf16[256,512]{1,0:T(8,128)(2,1)} %get-tuple-element.16), channel_id=1, source_target_pairs={{0,1},{1,0},{2,3},{3,2},{4,5},{5,4},{6,7},{7,6},{8,9},{9,8},{10,11... | collective-permute-start | bytes 786440 | tf_op jit(solution)/shard_map/ppermute | solution.py:288
  32.2 2.5 %collective-permute-start.2 = (bf16[256,512]{1,0:T(8,128)(2,1)}, bf16[256,512]{1,0:T(8,128)(2,1)S(1)}, u32[]{:S(2)}, u32[]{:S(2)}) collective-permute-start(bf16[256,512]{1,0:T(8,128)(2,1)} %get-tuple-element.17), channel_id=1, source_target_pairs={{0,3},{1,2},{2,1},{3,0},{4,7},{5,6},{6,5},{7,4},{8,11},{9,10},{10,... | collective-permute-start | bytes 786440 | tf_op jit(solution)/shard_map/ppermute | solution.py:288
  34.7 1.0 %all-to-all-done.got = bf16[128,2,384]{2,1,0:T(2,128)(2,1)S(1)} async-done(((bf16[128,2,384]{2,1,0:T(2,128)(2,1)}), bf16[128,2,384]{2,1,0:T(2,128)(2,1)S(1)}, u32[]{:S(2)}, u32[]{:S(2)}) %all-to-all-start) | async-done | bytes 196640 | tf_op jit(solution)/shard_map/all_to_all | solution.py:263
  35.6 1.6 %shard_map.143 = bf16[4,2,512]{2,1,0:T(2,128)(2,1)} custom-call(bf16[128,2,384]{2,1,0:T(2,128)(2,1)S(1)} %all-to-all-done.got, bf16[8,128]{1,0:T(8,128)(2,1)S(1)} %get-tuple-element.18.query, f32[8,128]{1,0:T(8,128)S(1)} %get-tuple-element.19.live, f32[8,128]{1,0:T(8,128)S(1)} %get-tuple-element.20.top_i, f32[8,128]{1,0:T(8,128)S(1)} %get-tuple-element.21.total_i, ...), custom_call_target="tpu_custom_call" | custom-call | tf_op jit(solution)/shard_map/pallas_call | solution.py:33
  37.2 4.0 %all-to-all-start.1 = ((bf16[4,2,512]{2,1,0:T(2,128)(2,1)}), bf16[4,2,512]{2,1,0:T(2,128)(2,1)S(1)}, u32[]{:S(2)}, u32[]{:S(2)}) async-start(bf16[4,2,512]{2,1,0:T(2,128)(2,1)} %shard_map.143), calls=%async_computation.1 | async-start | bytes 16384 | tf_op jit(solution)/shard_map/all_to_all | solution.py:297
  41.2 0.0 collective-permute-done.refs_1_
  41.2 0.3 collective-permute-done.1.refs_2_
  41.5 0.7 %collective-permute-done.2.refs_3_ = bf16[256,512]{1,0:T(8,128)(2,1)S(1)} collective-permute-done((bf16[256,512]{1,0:T(8,128)(2,1)}, bf16[256,512]{1,0:T(8,128)(2,1)S(1)}, u32[]{:S(2)}, u32[]{:S(2)}) %collective-permute-start.2) | collective-permute-done | bytes 262176 | tf_op jit(solution)/shard_map/ppermute | solution.py:288
  42.3 0.8 %shard_map.141 = bf16[256,512]{1,0:T(8,128)(2,1)} custom-call(bf16[256,512]{1,0:T(8,128)(2,1)S(1)} %get-tuple-element.14.refs_0_, bf16[256,512]{1,0:T(8,128)(2,1)S(1)} %collective-permute-done.refs_1_, bf16[256,512]{1,0:T(8,128)(2,1)S(1)} %collective-permute-done.1.refs_2_, bf16[256,512]{1,0:T(8,128)(2,1)S(1)} %collective-permute-done.2.refs_3_), custom_call_target="tpu_custom_call" | custom-call | tf_op jit(solution)/shard_map/pallas_call | solution.py:33
  43.1 2.3 %all-to-all-done.1 = bf16[4,2,512]{2,1,0:T(2,128)(2,1)S(1)} async-done(((bf16[4,2,512]{2,1,0:T(2,128)(2,1)}), bf16[4,2,512]{2,1,0:T(2,128)(2,1)S(1)}, u32[]{:S(2)}, u32[]{:S(2)}) %all-to-all-start.1) | async-done | bytes 8224 | tf_op jit(solution)/shard_map/all_to_all | solution.py:297
  45.4 0.6 %reduce_sum.12 = bf16[2,512]{1,0:T(2,128)(2,1)} reduce(bf16[4,2,512]{2,1,0:T(2,128)(2,1)S(1)} %all-to-all-done.1, bf16[]{:T(256)} %constant.4.clone.1), dimensions={0}, to_apply=%region_0.0 | reduce | flops 3072 | bytes 10242 | tf_op jit(solution)/shard_map/reduce_sum | solution.py:298
Async XLA Ops:
  3.3 32.3 %all-to-all-start = ((bf16[128,2,384]{2,1,0:T(2,128)(2,1)}), bf16[128,2,384]{2,1,0:T(2,128)(2,1)S(1)}, u32[]{:S(2)}, u32[]{:S(2)}) async-start(bf16[128,2,384]{2,1,0:T(2,128)(2,1)} %shard_map.142), calls=%async_computation | async-start | bytes 393216 | tf_op jit(solution)/shard_map/all_to_all | solution.py:263
  25.3 15.9 %collective-permute-start = (bf16[256,512]{1,0:T(8,128)(2,1)}, bf16[256,512]{1,0:T(8,128)(2,1)S(1)}, u32[]{:S(2)}, u32[]{:S(2)}) collective-permute-start(bf16[256,512]{1,0:T(8,128)(2,1)} %get-tuple-element.15), channel_id=1, source_target_pairs={{0,2},{1,3},{2,0},{3,1},{4,6},{5,7},{6,4},{7,5},{8,10},{9,11},{10,... | collective-permute-start | bytes 786440 | tf_op jit(solution)/shard_map/ppermute | solution.py:288
  30.0 11.6 %collective-permute-start.1 = (bf16[256,512]{1,0:T(8,128)(2,1)}, bf16[256,512]{1,0:T(8,128)(2,1)S(1)}, u32[]{:S(2)}, u32[]{:S(2)}) collective-permute-start(bf16[256,512]{1,0:T(8,128)(2,1)} %get-tuple-element.16), channel_id=1, source_target_pairs={{0,1},{1,0},{2,3},{3,2},{4,5},{5,4},{6,7},{7,6},{8,9},{9,8},{10,11... | collective-permute-start | bytes 786440 | tf_op jit(solution)/shard_map/ppermute | solution.py:288
  32.2 10.1 %collective-permute-start.2 = (bf16[256,512]{1,0:T(8,128)(2,1)}, bf16[256,512]{1,0:T(8,128)(2,1)S(1)}, u32[]{:S(2)}, u32[]{:S(2)}) collective-permute-start(bf16[256,512]{1,0:T(8,128)(2,1)} %get-tuple-element.17), channel_id=1, source_target_pairs={{0,3},{1,2},{2,1},{3,0},{4,7},{5,6},{6,5},{7,4},{8,11},{9,10},{10,... | collective-permute-start | bytes 786440 | tf_op jit(solution)/shard_map/ppermute | solution.py:288
  37.2 8.2 %all-to-all-start.1 = ((bf16[4,2,512]{2,1,0:T(2,128)(2,1)}), bf16[4,2,512]{2,1,0:T(2,128)(2,1)S(1)}, u32[]{:S(2)}, u32[]{:S(2)}) async-start(bf16[4,2,512]{2,1,0:T(2,128)(2,1)} %shard_map.143), calls=%async_computation.1 | async-start | bytes 16384 | tf_op jit(solution)/shard_map/all_to_all | solution.py:297

commit v5 on v4

--- a/solution.py
+++ b/solution.py
@@ -11,6 +11,7 @@
 CAP = 2
 ROPE_BASE = 600000.0
 VMEM_LIMIT = 16 * 2**20
+STRIDE = 37
 F32 = jnp.float32
 BF16 = jnp.bfloat16
 
@@ -54,7 +55,10 @@
     return pl.ds(pl.multiple_of(to * share, share), share)
 
 
-def pack_kernel(hidden, weight, dest, out, hidden_v, weight_v, dest_v, out_v, sem):
+def pack_kernel(
+    hidden, weight, dest, query, key_value, segment, out, query_o, key_value_o, segment_o,
+    hidden_v, weight_v, dest_v, out_v, sem, later_sem,
+):
     peers, cap, width = out.shape
     rows, depth = hidden.shape
     steps, halves = 4, 2
@@ -66,7 +70,8 @@
     )
     copies[0].wait()
     number = lax.broadcasted_iota(jnp.int32, (1, rows), 1)
-    code = dest_v[...] * cap + number % cap
+    member = ((peers - 1 - dest_v[...]) * pow(STRIDE, -1, peers)) % peers
+    code = member * cap + number % cap
     code = jnp.where(dest_v[...] >= 0, code, -1)
     place = lax.broadcasted_iota(jnp.int32, (peers * cap, rows), 0)
     chosen = jnp.where(place == code, 1.0, 0.0).astype(BF16)
@@ -76,6 +81,7 @@
         copies[2 + 2 * k].wait()
         rebuilt = rebuilt + dot(hidden_v[:, p], weight_v[p], 1, 0)
     rebuilt = rebuilt.astype(BF16)
+    later = start_all((query, key_value, segment), (query_o, key_value_o, segment_o), later_sem)
     sends = []
     for h in range(halves):
         size = peers // halves
@@ -85,30 +91,20 @@
         out_v[own] = jnp.concatenate([packed, mine], axis=1).reshape(size, cap, width)
         sends.append(pltpu.make_async_copy(out_v.at[own], out.at[own], sem.at[1 + 2 * steps + h]))
         sends[-1].start()
-    for send in sends:
-        send.wait()
+    for copy in sends + later:
+        copy.wait()
 
 
 def middle_kernel(parts, query, key_value, segment, weight, *refs):
-    blocks = 8
-    far, outs, weight_o = refs[:6], refs[6 : 13 + parts], refs[13 + parts]
-    held, sem = refs[14 + parts : 23 + parts], refs[23 + parts]
-    step = weight.shape[0] // blocks
-    block = [pl.ds(i * step, step) for i in range(blocks)]
-    copies = start_all(
-        [query, key_value, segment, *[weight.at[x] for x in block], *far],
-        [*held[:3], *[weight_o.at[x] for x in block], *held[3:]],
-        sem,
-    )
-    for copy in copies[:3]:
-        copy.wait()
-    mixed = prompt_rows(*held[:3])
-    for copy in copies[3:]:
-        copy.wait()
+    far, outs, held, sem = refs[:6], refs[6 : 13 + parts], refs[13 + parts : 19 + parts], refs[19 + parts]
+    copies = start_all(far, held, sem)
+    mixed = prompt_rows(query, key_value, segment)
     share = outs[0].shape[1]
     for k in range(parts):
-        outs[k][...] = dot(mixed, weight_o[:, columns_for(k, share, parts)], 1, 0).astype(BF16)
-    cache_rows(*held[3:], *outs[parts:])
+        outs[k][...] = dot(mixed, weight[:, columns_for(k, share, parts)], 1, 0).astype(BF16)
+    for copy in copies:
+        copy.wait()
+    cache_rows(*held, *outs[parts:])
 
 
 def prompt_rows(query, key_value, segment):
@@ -216,12 +212,13 @@
         out[t] = dot(mixed, weight[:, t * share : (t + 1) * share], 1, 0).astype(BF16)
 
 
-def sum_kernel(*refs):
-    *parts, out = refs
-    total = parts[0][...].astype(F32)
-    for part in parts[1:]:
+def sum_kernel(own, *refs):
+    *arrived, dec, prompt_out, dec_out = refs
+    total = own[...].astype(F32)
+    for part in arrived:
         total = total + part[...].astype(F32)
-    out[...] = total.astype(BF16)
+    prompt_out[...] = total.astype(BF16)
+    dec_out[...] = dec[...]
 
 
 def shards(
@@ -253,19 +250,20 @@
     rows = decoder_query.shape[1] // head * decoders
     payload = (peers, CAP, pair + listed)
     far = (rebuild_hidden_state, key_value_weight.reshape(-1, pair), owner_dest)
-    (send,) = call(
+    later = (prompt_query, prompt_key_value.reshape(tokens, pair), prompt_segment_index)
+    send, *kept = call(
         pack_kernel,
-        [shape(payload, BF16)],
-        far=far,
-        scratch=[*map(like, far), pltpu.VMEM(payload, BF16), pltpu.SemaphoreType.DMA((11,))],
+        [shape(payload, BF16), *map(like, later)],
+        far=far + later,
+        scratch=[*map(like, far), pltpu.VMEM(payload, BF16)]
+        + [pltpu.SemaphoreType.DMA((11,)), pltpu.SemaphoreType.DMA((3,))],
         far_out=1,
     )
-    got = lax.all_to_all(send, "req", split_axis=0, concat_axis=0, tiled=True)
+    members = [peers - 1 - (STRIDE * i) % peers for i in range(peers)]
+    got = lax.all_to_all(
+        send, "req", split_axis=0, concat_axis=0, tiled=True, axis_index_groups=[members]
+    )
     far = (
-        prompt_query,
-        prompt_key_value.reshape(tokens, pair),
-        prompt_segment_index,
-        out_weight,
         key_value_cache.reshape(-1, pair),
         live_cache_length.reshape(1, decoders),
         decoder_query,
@@ -278,10 +276,11 @@
         [pltpu.VMEM((tokens, share), BF16)] * parts
         + [pltpu.VMEM((rows, head), BF16), pltpu.VMEM((rows, listed), F32)]
         + [pltpu.VMEM((rows, head), F32)] * 3
-        + [pltpu.VMEM((listed, head), F32)] * 2
-        + [like(out_weight)],
+        + [pltpu.VMEM((listed, head), F32)] * 2,
+        *kept,
+        out_weight,
         far=far,
-        scratch=[like(x) for x in far if x is not out_weight] + [pltpu.SemaphoreType.DMA((17,))],
+        scratch=[*map(like, far), pltpu.SemaphoreType.DMA((len(far),))],
     )
     prompt_part, state = middle[:parts], middle[parts:]
     arrived = [
@@ -293,10 +292,18 @@
         [pltpu.VMEM((parts, decoders, share), BF16)],
         got,
         *state,
+        out_weight,
     )
     dec_got = lax.all_to_all(dec_part, "tp", split_axis=0, concat_axis=0, tiled=True)
     dec_out = jnp.sum(dec_got.astype(F32), axis=0).astype(BF16)
-    (prompt_out,) = call(sum_kernel, [shape((tokens, share), BF16)], prompt_part[0], *arrived)
+    own_part, dec_out = lax.optimization_barrier((prompt_part[0], dec_out))
+    prompt_out, dec_out = call(
+        sum_kernel,
+        [shape((tokens, share), BF16), shape((decoders, share), BF16)],
+        own_part,
+        *arrived,
+        dec_out,
+    )
     return prompt_out, dec_out
 
 

time: 46.3 us -> 45.6 us (0.985)
  the two profiles are of different devices: /device:TPU:1 before, /device:TPU:8 now
where the time goes in v5:
time: 45.6 us; the launch traced here: 45.3 us
  starting transfers between devices  27.7 us (61%)
  blocking collectives  9.31 us (20%)
  Pallas kernels  7.48 us (16%)
  between operations  0.73 us (2%)
    all_to_all x1, starting transfers between devices, shards(): lax.all_to_all(send, 'req', split_axis=0, concat_axis=0, tiled=True, axis...  17.8 us
    ppermute x3, starting transfers between devices, shards(): lax.ppermute(prompt_part[k], 'tp', [(i, i ^ k) for i in range(parts)])  9.92 us
    all_to_all x1, blocking collectives, shards(): lax.all_to_all(dec_part, 'tp', split_axis=0, concat_axis=0, tiled=True)  9.31 us
    pallas_call x4, Pallas kernels, call(): pl.pallas_call(kernel, out_shape=list(outs), in_specs=[vmem] * len(args)...  7.48 us
  transfers between devices with their start and end apart: 4, of which 0 were waited for; matrix products, arithmetic and copies ran while one was open for 0% of the time, Pallas kernels for 8%

profile of v5, /device:TPU:8, one launch (start us, length us, event | category | flops | bytes accessed | tf_op | source)
XLA Modules:
  0.0 45.3 jit_solution(9069305619446205275)
XLA Ops:
  0.6 0.0 copy-start
  0.6 2.8 %shard_map.140 = (bf16[128,2,384]{2,1,0:T(2,128)(2,1)}, bf16[256,512]{1,0:T(8,128)(2,1)S(1)}, bf16[256,256]{1,0:T(8,128)(2,1)S(1)}, s32[1,256]{1,0:T(1,128)S(1)}) custom-call(bf16[128,2048]{1,0:T(8,128)(2,1)} %hidden.1, bf16[2048,256]{1,0:T(8,128)(2,1)} %bitcast.5, s32[1,128]{1,0:T(1,128)} %dest.1, bf16[256,512]{1,0:T(8,128)(2,1)} %query.1, ...), custom_call_target="tpu_custom_call" | custom-call | tf_op jit(solution)/shard_map/pallas_call | solution.py:34
  3.5 17.8 %all-to-all-start = ((bf16[128,2,384]{2,1,0:T(2,128)(2,1)}), bf16[128,2,384]{2,1,0:T(2,128)(2,1)S(1)}, u32[]{:S(2)}, u32[]{:S(2)}) async-start(bf16[128,2,384]{2,1,0:T(2,128)(2,1)} %get-tuple-element.23), calls=%async_computation | async-start | bytes 393216 | tf_op jit(solution)/shard_map/all_to_all | solution.py:263
  21.3 0.0 copy-done
  21.3 2.8 %shard_map.141 = (bf16[256,512]{1,0:T(8,128)(2,1)S(1)}, bf16[256,512]{1,0:T(8,128)(2,1)}, bf16[256,512]{1,0:T(8,128)(2,1)}, bf16[256,512]{1,0:T(8,128)(2,1)}, bf...) custom-call(bf16[256,512]{1,0:T(8,128)(2,1)S(1)} %get-tuple-element., ...), custom_call_target="tpu_custom_call" | custom-call | tf_op jit(solution)/shard_map/pallas_call | solution.py:34
  24.2 4.9 %collective-permute-start = (bf16[256,512]{1,0:T(8,128)(2,1)}, bf16[256,512]{1,0:T(8,128)(2,1)S(1)}, u32[]{:S(2)}, u32[]{:S(2)}) collective-permute-start(bf16[256,512]{1,0:T(8,128)(2,1)} %get-tuple-element.32), channel_id=1, source_target_pairs={{0,2},{1,3},{2,0},{3,1},{4,6},{5,7},{6,4},{7,5},{8,10},{9,11},{10,... | collective-permute-start | bytes 786440 | tf_op jit(solution)/shard_map/ppermute | solution.py:287
  29.1 2.5 %collective-permute-start.1 = (bf16[256,512]{1,0:T(8,128)(2,1)}, bf16[256,512]{1,0:T(8,128)(2,1)S(1)}, u32[]{:S(2)}, u32[]{:S(2)}) collective-permute-start(bf16[256,512]{1,0:T(8,128)(2,1)} %get-tuple-element.33), channel_id=1, source_target_pairs={{0,1},{1,0},{2,3},{3,2},{4,5},{5,4},{6,7},{7,6},{8,9},{9,8},{10,11... | collective-permute-start | bytes 786440 | tf_op jit(solution)/shard_map/ppermute | solution.py:287
  31.6 2.5 %collective-permute-start.2 = (bf16[256,512]{1,0:T(8,128)(2,1)}, bf16[256,512]{1,0:T(8,128)(2,1)S(1)}, u32[]{:S(2)}, u32[]{:S(2)}) collective-permute-start(bf16[256,512]{1,0:T(8,128)(2,1)} %get-tuple-element.34), channel_id=1, source_target_pairs={{0,3},{1,2},{2,1},{3,0},{4,7},{5,6},{6,5},{7,4},{8,11},{9,10},{10,... | collective-permute-start | bytes 786440 | tf_op jit(solution)/shard_map/ppermute | solution.py:287
  34.1 0.0 all-to-all-done.got
  34.1 1.0 %shard_map.142 = bf16[4,2,512]{2,1,0:T(2,128)(2,1)S(1)} custom-call(bf16[128,2,384]{2,1,0:T(2,128)(2,1)S(1)} %all-to-all-done.got, bf16[8,128]{1,0:T(8,128)(2,1)S(1)} %get-tuple-element.24.query, f32[8,128]{1,0:T(8,128)S(1)} %get-tuple-element.25.live, f32[8,128]{1,0:T(8,128)S(1)} %get-tuple-element.26.top_i, f32[8,128]{1,0:T(8,128)S(1)} %get-tuple-element.27.total_i, ...), custom_call_target="tpu_custom_call" | custom-call | tf_op jit(solution)/shard_map/pallas_call | solution.py:34
  35.1 9.3 %all_to_all.10 = bf16[4,2,512]{2,1,0:T(2,128)(2,1)S(1)} all-to-all(bf16[4,2,512]{2,1,0:T(2,128)(2,1)S(1)} %shard_map.142), channel_id=1, replica_groups=mesh['req'=128,'tp'=4] {'tp'}, dimensions={0} | all-to-all | bytes 16384 | tf_op jit(solution)/shard_map/all_to_all | solution.py:297
  44.4 0.0 collective-permute-done.refs_0_
  44.4 0.0 collective-permute-done.1.refs_1_
  44.4 0.0 collective-permute-done.2.refs_2_
  44.4 0.8 %shard_map.143 = (bf16[256,512]{1,0:T(8,128)(2,1)}, bf16[2,512]{1,0:T(2,128)(2,1)}) custom-call(bf16[256,512]{1,0:T(8,128)(2,1)S(1)} %get-tuple-element.31.own, bf16[256,512]{1,0:T(8,128)(2,1)S(1)} %collective-permute-done.refs_0_, bf16[256,512]{1,0:T(8,128)(2,1)S(1)} %collective-permute-done.1.refs_1_, bf16[256,512]{1,0:T(8,128)(2,1)S(1)} %collective-permute-done.2.refs_2_, ...), custom_call_target="tpu_custom_call" | custom-call | tf_op jit(solution)/shard_map/pallas_call | solution.py:34
  (1 shorter events, 0.0 us)
Async XLA Ops:
  0.6 20.7 %copy-start = (bf16[512,2048]{1,0:T(8,128)(2,1)S(1)}, bf16[512,2048]{1,0:T(8,128)(2,1)}, u32[]{:S(2)}) copy-start(bf16[512,2048]{1,0:T(8,128)(2,1)} %weight.3) | copy-start | bytes 6291460
  3.5 30.6 %all-to-all-start = ((bf16[128,2,384]{2,1,0:T(2,128)(2,1)}), bf16[128,2,384]{2,1,0:T(2,128)(2,1)S(1)}, u32[]{:S(2)}, u32[]{:S(2)}) async-start(bf16[128,2,384]{2,1,0:T(2,128)(2,1)} %get-tuple-element.23), calls=%async_computation | async-start | bytes 393216 | tf_op jit(solution)/shard_map/all_to_all | solution.py:263
  24.2 20.2 %collective-permute-start = (bf16[256,512]{1,0:T(8,128)(2,1)}, bf16[256,512]{1,0:T(8,128)(2,1)S(1)}, u32[]{:S(2)}, u32[]{:S(2)}) collective-permute-start(bf16[256,512]{1,0:T(8,128)(2,1)} %get-tuple-element.32), channel_id=1, source_target_pairs={{0,2},{1,3},{2,0},{3,1},{4,6},{5,7},{6,4},{7,5},{8,10},{9,11},{10,... | collective-permute-start | bytes 786440 | tf_op jit(solution)/shard_map/ppermute | solution.py:287
  29.1 15.3 %collective-permute-start.1 = (bf16[256,512]{1,0:T(8,128)(2,1)}, bf16[256,512]{1,0:T(8,128)(2,1)S(1)}, u32[]{:S(2)}, u32[]{:S(2)}) collective-permute-start(bf16[256,512]{1,0:T(8,128)(2,1)} %get-tuple-element.33), channel_id=1, source_target_pairs={{0,1},{1,0},{2,3},{3,2},{4,5},{5,4},{6,7},{7,6},{8,9},{9,8},{10,11... | collective-permute-start | bytes 786440 | tf_op jit(solution)/shard_map/ppermute | solution.py:287
  31.6 12.8 %collective-permute-start.2 = (bf16[256,512]{1,0:T(8,128)(2,1)}, bf16[256,512]{1,0:T(8,128)(2,1)S(1)}, u32[]{:S(2)}, u32[]{:S(2)}) collective-permute-start(bf16[256,512]{1,0:T(8,128)(2,1)} %get-tuple-element.34), channel_id=1, source_target_pairs={{0,3},{1,2},{2,1},{3,0},{4,7},{5,6},{6,5},{7,4},{8,11},{9,10},{10,... | collective-permute-start | bytes 786440 | tf_op jit(solution)/shard_map/ppermute | solution.py:287
